TPU v7x, 32 devices: a whole 2x2x4 slice. The times are simulated.
32 devices in a mesh: dp: 8 (over y, x, core), tensor: 4 (over z).
Axes of the slice: x: 2, y: 2, z: 4, core: 2. Of those that a mesh axis runs over, the one named last changes fastest.
Arguments:
- tokens: bfloat16 [18432, 1024], P(('dp', 'tensor')), may hold values from -6 to 6
- cotangent: bfloat16 [18432, 1024], P(('dp', 'tensor')), may hold values from -6 to 6
- deal: int32 [18432], P(('dp', 'tensor')), may hold values from 0 to 18431, as said below
- source: int32 [18432], P(('dp', 'tensor')), may hold values from 0 to 18431, as said below
- lengths: int32 [8, 2, 3], P('dp'), may hold values from 1 to 1024, 1152 in all within a row
- qkv_weight: bfloat16 [3, 1024, 1024], P(None, 'dp', 'tensor'), may hold values from -0.1875 to 0.1875
- query_bias: bfloat16 [1024], replicated, may hold values from -3 to 3
- value_bias: bfloat16 [1024], replicated, may hold values from -3 to 3
- out_weight: bfloat16 [1024, 1024], P('tensor', 'dp'), may hold values from -3 to 3
- out_bias: bfloat16 [1024], replicated, may hold values from -3 to 3
- first_gain: bfloat16 [1024], replicated, may hold values from 0.5 to 1.5
- first_shift: bfloat16 [1024], replicated, may hold values from -3 to 3
- up_weight: bfloat16 [1024, 4096], P('dp', 'tensor'), may hold values from -0.1875 to 0.1875
- up_bias: bfloat16 [4096], replicated, may hold values from -3 to 3
- down_weight: bfloat16 [4096, 1024], P('tensor', 'dp'), may hold values from -0.09375 to 0.09375
- down_bias: bfloat16 [1024], replicated, may hold values from -3 to 3
- second_gain: bfloat16 [1024], replicated, may hold values from 0.5 to 1.5
- second_shift: bfloat16 [1024], replicated, may hold values from -3 to 3
Outputs:
- layer_out: bfloat16 [18432, 1024], P(('dp', 'tensor'))
- tokens_grad: float32 [18432, 1024], P(('dp', 'tensor'))
- qkv_grad: float32 [3, 1024, 1024], P(None, 'dp', 'tensor')
- query_bias_grad: float32 [1024], replicated
- value_bias_grad: float32 [1024], replicated
- out_weight_grad: float32 [1024, 1024], P('tensor', 'dp')
- out_bias_grad: float32 [1024], replicated
- first_gain_grad: float32 [1024], replicated
- first_shift_grad: float32 [1024], replicated
- up_weight_grad: float32 [1024, 4096], P('dp', 'tensor')
- up_bias_grad: float32 [4096], replicated
- down_weight_grad: float32 [4096, 1024], P('tensor', 'dp')
- down_bias_grad: float32 [1024], replicated
- second_gain_grad: float32 [1024], replicated
- second_shift_grad: float32 [1024], replicated
Inputs may be any that keep to these rules, and one draw needn't show every extreme that they name: A permutation: given row g becomes work row deal[g]. The given rows of an aligned block of 576 with block index c all go to blocks of 576 work rows whose index has the same remainder as c modulo 4, exactly 72 rows into each of them. The inverse of deal: source[deal[g]] = g.
All inputs are finite; a program needn't handle non-finite values.
Results may differ from a plain program's by a relative error of at most 0.014.
The roundings to bfloat16 on the way count: a program that leaves them out, or rounds other values in their place, can miss the bound.
Values may be sent and summed in bfloat16 or wider, within the bound.
A program may use at most 256 MiB of HBM per device.

v0:
```python
import jax
import jax.numpy as jnp
from jax import lax
from jax.sharding import PartitionSpec as P

DH = 64
MB = 2


def layer_norm(values, gain_vec, shift_vec):
    center = values - jnp.mean(values, axis=-1, keepdims=True)
    spread = jnp.mean(center * center, axis=-1, keepdims=True)
    return center * lax.rsqrt(spread + 1e-05) * gain_vec + shift_vec


def gelu_exact(values):
    return jax.nn.gelu(values, approximate=False)


def spread_rows(rows_local):
    return lax.all_gather(rows_local, "tensor", axis=0, tiled=True)


def collect_feed(partial_rows):
    return lax.psum_scatter(partial_rows, "tensor", scatter_dimension=0, tiled=True)


def spread_grads(rows_local):
    return lax.all_gather(rows_local, "tensor", axis=0, tiled=True)


def collect_grads(partial_rows):
    return lax.psum_scatter(partial_rows, "tensor", scatter_dimension=0, tiled=True)


def attention_projection(mixed_heads, out_full):
    out_part = jnp.dot(mixed_heads, out_full, preferred_element_type=jnp.float32)
    return lax.psum_scatter(out_part, "tensor", scatter_dimension=0, tiled=True)


def masked_scores(queries, key_rows, allowed, scale):
    raw_scores = (
        jnp.einsum("qhd,khd->hqk", queries, key_rows, preferred_element_type=jnp.float32) * scale
    )
    return jnp.where(allowed[None], raw_scores, -1e30)


def on_device(
    tokens,
    cotangent,
    deal,
    source,
    lengths,
    qkv_weight,
    query_bias,
    value_bias,
    out_weight,
    out_bias,
    first_gain,
    first_shift,
    up_weight,
    up_bias,
    down_weight,
    down_bias,
    second_gain,
    second_shift,
):
    float_kind = jnp.float32
    brain_kind = jnp.bfloat16
    row_count = tokens.shape[0]
    width = tokens.shape[1]
    data_ways = lax.axis_size("dp")
    split_ways = lax.axis_size("tensor")
    split_index = lax.axis_index("tensor")
    per_peer = row_count // data_ways
    group_rows = split_ways * row_count
    quarter = row_count // MB
    batch_rows = split_ways * quarter
    local_width = qkv_weight.shape[2]
    local_hidden = up_weight.shape[1]
    head_count = local_width // DH
    scale = DH ** (-0.5)
    targets = deal // group_rows
    one_hot = (targets[:, None] == jnp.arange(data_ways, dtype=jnp.int32)[None, :]).astype(
        jnp.int32
    )
    send_slot = targets * per_peer + jnp.sum(one_hot * jnp.cumsum(one_hot, axis=0), axis=1) - 1
    outgoing_x = jnp.zeros_like(tokens).at[send_slot].set(tokens)
    outgoing_g = jnp.zeros_like(cotangent).at[send_slot].set(cotangent)
    arrived_x, arrived_g = (
        lax.all_to_all(outgoing_x, "dp", split_axis=0, concat_axis=0, tiled=True),
        lax.all_to_all(outgoing_g, "dp", split_axis=0, concat_axis=0, tiled=True),
    )
    senders = source // group_rows
    earlier = (senders[:, None] == senders[None, :]) & (source[None, :] < source[:, None])
    recv_slot = senders * per_peer + jnp.sum(earlier.astype(jnp.int32), axis=1)
    work_x = arrived_x[recv_slot]
    work_g = arrived_g[recv_slot]
    query_local = lax.dynamic_slice_in_dim(
        query_bias.astype(float_kind), split_index * local_width, local_width
    )
    value_local = lax.dynamic_slice_in_dim(
        value_bias.astype(float_kind), split_index * local_width, local_width
    )
    up_local = lax.dynamic_slice_in_dim(
        up_bias.astype(float_kind), split_index * local_hidden, local_hidden
    )
    out_bias_f = out_bias.astype(float_kind)
    down_bias_f = down_bias.astype(float_kind)
    first_gain_f = first_gain.astype(float_kind)
    first_shift_f = first_shift.astype(float_kind)
    second_gain_f = second_gain.astype(float_kind)
    second_shift_f = second_shift.astype(float_kind)

    def fetch_attention():
        return (
            lax.all_gather(qkv_weight, "dp", axis=1, tiled=True),
            lax.all_gather(out_weight, "dp", axis=1, tiled=True),
        )

    def fetch_feed():
        return (
            lax.all_gather(up_weight, "dp", axis=0, tiled=True),
            lax.all_gather(down_weight, "dp", axis=1, tiled=True),
        )

    acc_qkv = jnp.zeros((3, width, local_width), float_kind)
    acc_out = jnp.zeros((local_width, width), float_kind)
    acc_up = jnp.zeros((width, local_hidden), float_kind)
    acc_down = jnp.zeros((local_hidden, width), float_kind)
    acc_query_bias = jnp.zeros((local_width,), float_kind)
    acc_value_bias = jnp.zeros((local_width,), float_kind)
    acc_up_bias = jnp.zeros((local_hidden,), float_kind)
    acc_out_bias = jnp.zeros((width,), float_kind)
    acc_down_bias = jnp.zeros((width,), float_kind)
    acc_first_gain = jnp.zeros((width,), float_kind)
    acc_first_shift = jnp.zeros((width,), float_kind)
    acc_second_gain = jnp.zeros((width,), float_kind)
    acc_second_shift = jnp.zeros((width,), float_kind)
    positions = jnp.arange(batch_rows, dtype=jnp.int32)
    result_parts = []
    input_parts = []
    for batch_index in range(MB):
        inputs_local = work_x[batch_index * quarter : (batch_index + 1) * quarter]
        grad_local = work_g[batch_index * quarter : (batch_index + 1) * quarter].astype(float_kind)
        seq_ends = jnp.cumsum(lengths[0, batch_index])
        seq_ids = jnp.sum((positions[:, None] >= seq_ends[None, :]).astype(jnp.int32), axis=1)
        allowed = seq_ids[:, None] == seq_ids[None, :]
        qkv_full, out_full = fetch_attention()
        inputs_full = spread_rows(inputs_local)
        projected = jnp.einsum(
            "td,cde->cte", inputs_full, qkv_full, preferred_element_type=float_kind
        )
        queries = (
            (projected[0] + query_local).astype(brain_kind).reshape(batch_rows, head_count, DH)
        )
        key_rows = projected[1].astype(brain_kind).reshape(batch_rows, head_count, DH)
        value_rows = (
            (projected[2] + value_local).astype(brain_kind).reshape(batch_rows, head_count, DH)
        )
        scores = masked_scores(queries, key_rows, allowed, scale)
        row_max = jnp.max(scores, axis=-1, keepdims=True)
        log_total = row_max + jnp.log(jnp.sum(jnp.exp(scores - row_max), axis=-1, keepdims=True))
        probs_low = jnp.exp(scores - log_total).astype(brain_kind)
        mixed_heads = (
            jnp.einsum("hqk,khd->qhd", probs_low, value_rows, preferred_element_type=float_kind)
            .astype(brain_kind)
            .reshape(batch_rows, local_width)
        )
        first_sum = (
            inputs_local.astype(float_kind)
            + attention_projection(mixed_heads, out_full)
            + out_bias_f
        )
        normed, first_pull = jax.vjp(layer_norm, first_sum, first_gain_f, first_shift_f)
        normed_full = spread_rows(normed.astype(brain_kind))
        up_full, down_full = fetch_feed()
        pre_act = jnp.dot(normed_full, up_full, preferred_element_type=float_kind) + up_local
        activated, gelu_pull = jax.vjp(gelu_exact, pre_act)
        hidden = activated.astype(brain_kind)
        down_part = jnp.dot(hidden, down_full, preferred_element_type=float_kind)
        second_sum = normed + collect_feed(down_part) + down_bias_f
        result, second_pull = jax.vjp(layer_norm, second_sum, second_gain_f, second_shift_f)
        result_parts.append(result)
        second_back, second_gain_back, second_shift_back = second_pull(grad_local)
        acc_second_gain = acc_second_gain + second_gain_back
        acc_second_shift = acc_second_shift + second_shift_back
        acc_down_bias = acc_down_bias + jnp.sum(second_back, axis=0)
        up_full, down_full = fetch_feed()
        down_incoming = spread_grads(second_back.astype(brain_kind))
        acc_down = acc_down + jnp.einsum(
            "tf,td->fd", hidden, down_incoming, preferred_element_type=float_kind
        )
        hidden_back = jnp.einsum(
            "td,fd->tf", down_incoming, down_full, preferred_element_type=float_kind
        )
        (pre_back,) = gelu_pull(hidden_back)
        acc_up_bias = acc_up_bias + jnp.sum(pre_back, axis=0)
        pre_low = pre_back.astype(brain_kind)
        acc_up = acc_up + jnp.einsum(
            "td,tf->df", normed_full, pre_low, preferred_element_type=float_kind
        )
        normed_part = jnp.einsum("tf,df->td", pre_low, up_full, preferred_element_type=float_kind)
        normed_back = second_back + collect_grads(normed_part)
        first_back, first_gain_back, first_shift_back = first_pull(normed_back)
        acc_first_gain = acc_first_gain + first_gain_back
        acc_first_shift = acc_first_shift + first_shift_back
        acc_out_bias = acc_out_bias + jnp.sum(first_back, axis=0)
        qkv_full, out_full = fetch_attention()
        out_incoming = spread_grads(first_back.astype(brain_kind))
        acc_out = acc_out + jnp.einsum(
            "tc,td->cd", mixed_heads, out_incoming, preferred_element_type=float_kind
        )
        mixed_back = jnp.einsum(
            "td,cd->tc", out_incoming, out_full, preferred_element_type=float_kind
        )
        mixed_back = mixed_back.astype(brain_kind).reshape(batch_rows, head_count, DH)
        value_back = jnp.einsum(
            "hqk,qhd->khd", probs_low, mixed_back, preferred_element_type=float_kind
        ).reshape(batch_rows, local_width)
        prob_back = jnp.einsum(
            "qhd,khd->hqk", mixed_back, value_rows, preferred_element_type=float_kind
        )
        again = masked_scores(queries, key_rows, allowed, scale)
        row_dot = jnp.sum(prob_back * jnp.exp(again - log_total), axis=-1, keepdims=True)
        score_back = (jnp.exp(again - log_total) * (prob_back - row_dot) * scale).astype(brain_kind)
        query_back = jnp.einsum(
            "hqk,khd->qhd", score_back, key_rows, preferred_element_type=float_kind
        ).reshape(batch_rows, local_width)
        key_back = jnp.einsum(
            "hqk,qhd->khd", score_back, queries, preferred_element_type=float_kind
        ).reshape(batch_rows, local_width)
        acc_query_bias = acc_query_bias + jnp.sum(query_back, axis=0)
        acc_value_bias = acc_value_bias + jnp.sum(value_back, axis=0)
        proj_back = jnp.stack([query_back, key_back, value_back]).astype(brain_kind)
        acc_qkv = acc_qkv + jnp.einsum(
            "td,cte->cde", inputs_full, proj_back, preferred_element_type=float_kind
        )
        input_part = jnp.einsum(
            "cte,cde->td", proj_back, qkv_full, preferred_element_type=float_kind
        )
        input_parts.append(first_back + collect_grads(input_part))
    layer_work = jnp.concatenate(result_parts, axis=0)
    input_work = jnp.concatenate(input_parts, axis=0)
    back_layer = jnp.zeros((row_count, width), float_kind).at[recv_slot].set(layer_work)
    back_input = jnp.zeros((row_count, width), float_kind).at[recv_slot].set(input_work)
    returned_layer, returned_input = (
        lax.all_to_all(
            back_layer.astype(jnp.bfloat16), "dp", split_axis=0, concat_axis=0, tiled=True
        ).astype(back_layer.dtype),
        lax.all_to_all(
            back_input.astype(jnp.bfloat16), "dp", split_axis=0, concat_axis=0, tiled=True
        ).astype(back_input.dtype),
    )
    layer_out = returned_layer[send_slot].astype(brain_kind)
    tokens_grad = returned_input[send_slot]
    qkv_grad, out_weight_grad, up_weight_grad, down_weight_grad = (
        lax.psum_scatter(acc_qkv, "dp", scatter_dimension=1, tiled=True),
        lax.psum_scatter(acc_out, "dp", scatter_dimension=1, tiled=True),
        lax.psum_scatter(acc_up, "dp", scatter_dimension=0, tiled=True),
        lax.psum_scatter(acc_down, "dp", scatter_dimension=1, tiled=True),
    )
    query_placed = lax.dynamic_update_slice_in_dim(
        jnp.zeros((width,), float_kind), acc_query_bias, split_index * local_width, 0
    )
    value_placed = lax.dynamic_update_slice_in_dim(
        jnp.zeros((width,), float_kind), acc_value_bias, split_index * local_width, 0
    )
    up_placed = lax.dynamic_update_slice_in_dim(
        jnp.zeros((split_ways * local_hidden,), float_kind),
        acc_up_bias,
        split_index * local_hidden,
        0,
    )
    (
        query_bias_grad,
        value_bias_grad,
        out_bias_grad,
        first_gain_grad,
        first_shift_grad,
        up_bias_grad,
        down_bias_grad,
        second_gain_grad,
        second_shift_grad,
    ) = lax.psum(
        (
            query_placed,
            value_placed,
            acc_out_bias,
            acc_first_gain,
            acc_first_shift,
            up_placed,
            acc_down_bias,
            acc_second_gain,
            acc_second_shift,
        ),
        ("dp", "tensor"),
    )
    return (
        layer_out,
        tokens_grad,
        qkv_grad,
        query_bias_grad,
        value_bias_grad,
        out_weight_grad,
        out_bias_grad,
        first_gain_grad,
        first_shift_grad,
        up_weight_grad,
        up_bias_grad,
        down_weight_grad,
        down_bias_grad,
        second_gain_grad,
        second_shift_grad,
    )


def solution(mesh):
    in_specs = (
        P(("dp", "tensor"), None),
        P(("dp", "tensor"), None),
        P(("dp", "tensor")),
        P(("dp", "tensor")),
        P("dp", None, None),
        P(None, "dp", "tensor"),
        P(),
        P(),
        P("tensor", "dp"),
        P(),
        P(),
        P(),
        P("dp", "tensor"),
        P(),
        P("tensor", "dp"),
        P(),
        P(),
        P(),
    )
    out_specs = (
        P(("dp", "tensor"), None),
        P(("dp", "tensor"), None),
        P(None, "dp", "tensor"),
        P(),
        P(),
        P("tensor", "dp"),
        P(),
        P(),
        P(),
        P("dp", "tensor"),
        P(),
        P("tensor", "dp"),
        P(),
        P(),
        P(),
    )
    return jax.shard_map(
        on_device, mesh=mesh, in_specs=in_specs, out_specs=out_specs, check_vma=False
    )
```

profile of v0, /device:TPU:1, one launch (start us, length us, event | category | flops | bytes accessed | tf_op | source)
XLA Modules:
  0.0 1503.0 jit_solution(10362224496821400069)
XLA Ops:
  25.6 17.0 %all-to-all-done = bf16[8,72,1024]{2,1,0:T(8,128)(2,1)S(1)} async-done(((bf16[8,72,1024]{2,1,0:T(8,128)(2,1)}), bf16[8,72,1024]{2,1,0:T(8,128)(2,1)S(1)}, u32[]{:S(2)}, u32[]{:S(2)}) %all-to-all-start) | async-done | bytes 1179680 | tf_op jit(solution)/shard_map/all_to_all | solution.py:91
  47.3 13.4 all_gather.50
  61.9 37.6 %all-gather.12.cloned.1.call-done = bf16[1152,1024]{1,0:T(8,128)(2,1)} async-done(((bf16[288,1024]{1,0:T(8,128)(2,1)}), bf16[1152,1024]{1,0:T(8,128)(2,1)}) %all-gather.12.cloned.1.call-update) | async-done | bytes 2359312 | tf_op jit(solution)/shard_map/all_gather | solution.py:21
  135.1 15.2 %all-gather.22.cloned.1.call-done = bf16[1152,1024]{1,0:T(8,128)(2,1)} async-done(((bf16[288,1024]{1,0:T(8,128)(2,1)}), bf16[1152,1024]{1,0:T(8,128)(2,1)}) %all-gather.22.cloned.1.call-update) | async-done | bytes 2359312 | tf_op jit(solution)/shard_map/all_gather | solution.py:21
  170.0 10.6 fusion.65
  186.1 50.6 %reduce-scatter.13.cloned.1.call-done = f32[288,1024]{1,0:T(8,128)} async-done(((f32[1152,1024]{1,0:T(8,128)}), f32[288,1024]{1,0:T(8,128)}) %reduce-scatter.13.cloned.1.call-update) | async-done | bytes 1179664 | tf_op jit(solution)/shard_map/reduce_scatter | solution.py:38
  236.7 88.0 %reduce-scatter.17.cloned.1.call-done = f32[288,1024]{1,0:T(8,128)} async-done(((f32[1152,1024]{1,0:T(8,128)}), f32[288,1024]{1,0:T(8,128)}) %reduce-scatter.17.cloned.1.call-update) | async-done | bytes 1179664 | tf_op jit(solution)/shard_map/reduce_scatter | solution.py:38
  330.8 24.5 %all-gather.18.cloned.1.call-done = bf16[1024,1024]{1,0:T(8,128)(2,1)} async-done(((bf16[128,1024]{1,0:T(8,128)(2,1)}), bf16[1024,1024]{1,0:T(8,128)(2,1)}) %all-gather.18.cloned.1.call-update) | async-done | bytes 2097168 | tf_op jit(solution)/shard_map/all_gather | solution.py:123
  355.2 52.2 %all-gather.24.cloned.1.call-done = bf16[1152,1024]{1,0:T(8,128)(2,1)} async-done(((bf16[288,1024]{1,0:T(8,128)(2,1)}), bf16[1152,1024]{1,0:T(8,128)(2,1)}) %all-gather.24.cloned.1.call-update) | async-done | bytes 2359312 | tf_op jit(solution)/shard_map/all_gather | solution.py:21
  407.4 16.2 %multiply_convert_fusion = (bf16[1152,1024]{1,0:T(8,128)(2,1)}, f32[1152,1024]{1,0:T(8,128)}, f32[1152,1024]{1,0:T(8,128)}) fusion(f32[1024]{0:T(1024)S(1)} %dynamic-slice_convert_fusion, bf16[1152,1024]{1,0:T(8,128)(2,1)} %all-gather.24.cloned.1.call-done, bf16[1024,1024]{1,0:T(8,128)(2,1)} %all-gather.18.cloned.1.call-done), kind=kOutput, calls=%fused_computation.44 | convolution fusion | flops 2493775872 | bytes 16257024 | tf_op jit(solution)/shard_map/dot_general | solution.py:178
  423.6 13.2 all-gather.20.cloned.1.call-done
  444.2 44.8 %all-gather.16.cloned.1.call-done = bf16[1152,1024]{1,0:T(8,128)(2,1)} async-done(((bf16[288,1024]{1,0:T(8,128)(2,1)}), bf16[1152,1024]{1,0:T(8,128)(2,1)}) %all-gather.16.cloned.1.call-update) | async-done | bytes 2359312 | tf_op jit(solution)/shard_map/all_gather | solution.py:21
  489.0 16.1 %multiply_convert_fusion.1 = (bf16[1152,1024]{1,0:T(8,128)(2,1)S(1)}, f32[1152,1024]{1,0:T(8,128)}, f32[1152,1024]{1,0:T(8,128)}) fusion(f32[1024]{0:T(1024)S(1)} %dynamic-slice_convert_fusion, bf16[1152,1024]{1,0:T(8,128)(2,1)} %all-gather.16.cloned.1.call-done, bf16[1024,1024]{1,0:T(8,128)(2,1)} %all-gather.18.cloned.1.call-done), kind=kOutput, calls=%fused_computation.57 | convolution fusion | flops 2493775872 | bytes 16257024 | tf_op jit(solution)/shard_map/dot_general | solution.py:178
  539.6 35.8 %reduce-scatter.19.cloned.1.call-done = f32[288,1024]{1,0:T(8,128)} async-done(((f32[1152,1024]{1,0:T(8,128)}), f32[288,1024]{1,0:T(8,128)}) %reduce-scatter.19.cloned.1.call-update) | async-done | bytes 1179664 | tf_op jit(solution)/shard_map/reduce_scatter | solution.py:25
  575.4 88.1 %reduce-scatter.15.cloned.1.call-done = f32[288,1024]{1,0:T(8,128)} async-done(((f32[1152,1024]{1,0:T(8,128)}), f32[288,1024]{1,0:T(8,128)}) %reduce-scatter.15.cloned.1.call-update) | async-done | bytes 1179664 | tf_op jit(solution)/shard_map/reduce_scatter | solution.py:25
  678.2 46.8 %all-gather.30.cloned.1.call-done = bf16[1152,1024]{1,0:T(8,128)(2,1)} async-done(((bf16[288,1024]{1,0:T(8,128)(2,1)}), bf16[1152,1024]{1,0:T(8,128)(2,1)}) %all-gather.30.cloned.1.call-update) | async-done | bytes 2359312 | tf_op jit(solution)/shard_map/all_gather | solution.py:29
  741.0 34.8 %all-gather.26.cloned.1.call-done = bf16[1152,1024]{1,0:T(8,128)(2,1)} async-done(((bf16[288,1024]{1,0:T(8,128)(2,1)}), bf16[1152,1024]{1,0:T(8,128)(2,1)}) %all-gather.26.cloned.1.call-update) | async-done | bytes 2359312 | tf_op jit(solution)/shard_map/all_gather | solution.py:29
  791.5 70.7 %reduce-scatter.25.cloned.1.call-done = f32[288,1024]{1,0:T(8,128)} async-done(((f32[1152,1024]{1,0:T(8,128)}), f32[288,1024]{1,0:T(8,128)}) %reduce-scatter.25.cloned.1.call-update) | async-done | bytes 1179664 | tf_op jit(solution)/shard_map/reduce_scatter | solution.py:33
  862.2 88.0 %reduce-scatter.21.cloned.1.call-done = f32[288,1024]{1,0:T(8,128)} async-done(((f32[1152,1024]{1,0:T(8,128)}), f32[288,1024]{1,0:T(8,128)}) %reduce-scatter.21.cloned.1.call-update) | async-done | bytes 1179664 | tf_op jit(solution)/shard_map/reduce_scatter | solution.py:33
  961.7 49.3 %all-gather.28.cloned.1.call-done = bf16[1152,1024]{1,0:T(8,128)(2,1)} async-done(((bf16[288,1024]{1,0:T(8,128)(2,1)}), bf16[1152,1024]{1,0:T(8,128)(2,1)}) %all-gather.28.cloned.1.call-update) | async-done | bytes 2359312 | tf_op jit(solution)/shard_map/all_gather | solution.py:29
  1013.7 12.0 fusion.149
  1026.7 11.3 fusion.113
  1038.0 30.5 %fusion.151 = (f32[4,64]{1,0:T(4,128)}, bf16[1152,4,64]{0,2,1:T(8,128)(2,1)}) fusion(bf16[1152,4,64]{0,2,1:T(8,128)(2,1)S(1)} %bitcast.152, f32[4,1152,1152]{1,2,0:T(8,128)} %fusion.113, f32[4,1152,1152]{1,2,0:T(8,128)} %copy-done.1, f32[4,1152]{1,0:T(4,128)S(1)} %copy-done.38), kind=kOutput, calls=%fused_computation.261 | convolution fusion | flops 717231488 | bytes 43666432 | tf_op jit(solution)/shard_map/hqk,khd->qhd/dot_general | solution.py:227
  1070.6 28.8 %fusion.71 = bf16[4,64,1152]{2,1,0:T(8,128)(2,1)} fusion(f32[4,1152,1152]{1,2,0:T(8,128)} %fusion.113, f32[4,1152,1152]{1,2,0:T(8,128)} %copy-done.1, f32[4,1152]{1,0:T(4,128)S(1)} %copy-done.38, f32[1152,4,64]{0,2,1:T(8,128)S(1)} %bitcast.147, f32[4,64]{1,0:T(4,128)S(1)} %copy-done.35), kind=kOutput, calls=%fused_computation.92 | convolution fusion | flops 717526656 | bytes 44256256 | tf_op jit(solution)/shard_map/hqk,qhd->khd/dot_general | solution.py:230
  1109.4 12.1 fusion.148
  1131.9 33.7 %fusion.150 = (f32[4,64]{1,0:T(4,128)}, bf16[1152,4,64]{0,2,1:T(8,128)(2,1)S(1)}) fusion(bf16[1152,4,64]{0,2,1:T(8,128)(2,1)S(1)} %bitcast.154, f32[4,1152,1152]{1,2,0:T(8,128)} %fusion.114, f32[4,1152,1152]{1,2,0:T(8,128)} %copy-done, f32[4,1152]{1,0:T(4,128)} %copy-done.36), kind=kOutput, calls=%fused_computation.260 | convolution fusion | flops 717231488 | bytes 43666432 | tf_op jit(solution)/shard_map/hqk,khd->qhd/dot_general | solution.py:227
  1165.8 34.5 %fusion.68 = bf16[4,64,1152]{2,1,0:T(8,128)(2,1)} fusion(f32[4,1152,1152]{1,2,0:T(8,128)} %fusion.114, f32[4,1152,1152]{1,2,0:T(8,128)} %copy-done, f32[4,1152]{1,0:T(4,128)} %copy-done.36, f32[1152,4,64]{0,2,1:T(8,128)S(1)} %bitcast.145, f32[4,64]{1,0:T(4,128)S(1)} %copy-done.35), kind=kOutput, calls=%fused_computation.91 | convolution fusion | flops 717526656 | bytes 44256256 | tf_op jit(solution)/shard_map/hqk,qhd->khd/dot_general | solution.py:230
  1257.1 34.5 %reduce-scatter.27.cloned.1.call-done = f32[288,1024]{1,0:T(8,128)} async-done(((f32[1152,1024]{1,0:T(8,128)}), f32[288,1024]{1,0:T(8,128)}) %reduce-scatter.27.cloned.1.call-update) | async-done | bytes 1179664 | tf_op jit(solution)/shard_map/reduce_scatter | solution.py:33
  1311.8 48.1 %all-reduce.1 = (f32[1024]{0:T(1024)}, f32[1024]{0:T(1024)}, f32[1024]{0:T(1024)}, f32[1024]{0:T(1024)}, f32[1024]{0:T(1024)}, /*index=5*/f32[4096]{0:T(1024)}, f32[1024]{0:T(1024)}, f32[1024]{0:T(1024)}, f32[1024]{0:T(1024)}) all-reduce(f32[1024]{0:T(1024)S(1)} %dynamic_update_slice.9, ...), channel_id=1, replica_groups=mesh['dp'=8,'tensor'=4] {'dp','tensor'}, use_global_device_ids=true, to_apply=%region_45.46 | all-reduce | flops 12288 | bytes 98304 | tf_op jit(solution)/shard_map/psum | solution.py:285
  1365.6 35.4 %reduce-scatter.35.cloned.1.call-done = f32[1024,128]{1,0:T(8,128)} async-done(((f32[1024,1024]{1,0:T(8,128)}), f32[1024,128]{1,0:T(8,128)}) %reduce-scatter.35.cloned.1.call-update) | async-done | bytes 524304 | tf_op jit(solution)/shard_map/reduce_scatter | solution.py:261
  1401.0 55.3 %reduce-scatter.33.cloned.1.call-done = f32[128,1024]{1,0:T(8,128)} async-done(((f32[1024,1024]{1,0:T(8,128)}), f32[128,1024]{1,0:T(8,128)}) %reduce-scatter.33.cloned.1.call-update) | async-done | bytes 524304 | tf_op jit(solution)/shard_map/reduce_scatter | solution.py:260
  1456.2 40.0 %reduce-scatter.31.cloned.1.call-done = f32[256,128]{1,0:T(8,128)} async-done(((f32[256,1024]{1,0:T(8,128)}), f32[256,128]{1,0:T(8,128)}) %reduce-scatter.31.cloned.1.call-update) | async-done | bytes 131088 | tf_op jit(solution)/shard_map/reduce_scatter | solution.py:259
  (373 shorter events, 298.4 us)
Async XLA Ops:
  7.2 54.7 %all-gather.14.cloned.1.call-start = ((), (), s32[]{:S(2)}) async-start(), calls=%async_computation.17 | async-start | bytes 1769472 | tf_op jit(solution)/shard_map/all_gather | solution.py:117
  19.9 22.8 %all-to-all-start = ((bf16[8,72,1024]{2,1,0:T(8,128)(2,1)}), bf16[8,72,1024]{2,1,0:T(8,128)(2,1)S(1)}, u32[]{:S(2)}, u32[]{:S(2)}) async-start(bf16[8,72,1024]{2,1,0:T(8,128)(2,1)} %bitcast.4), calls=%async_computation | async-start | bytes 2359296 | tf_op jit(solution)/shard_map/all_to_all | solution.py:91
  25.1 74.4 %all-gather.12.cloned.1.call-start = ((), (), s32[]{:S(2)}) async-start(), calls=%async_computation.16 | async-start | bytes 2949120 | tf_op jit(solution)/shard_map/all_gather | solution.py:21
  46.7 103.7 %all-gather.22.cloned.1.call-start = ((), (), s32[]{:S(2)}) async-start(), calls=%async_computation.23 | async-start | bytes 2949120 | tf_op jit(solution)/shard_map/all_gather | solution.py:21
  46.9 109.8 %copy-start.34 = (f32[4,64]{1,0:T(4,128)}, f32[4,64]{1,0:T(4,128)S(1)}, u32[]{:S(2)}) copy-start(f32[4,64]{1,0:T(4,128)S(1)} %add.320) | copy-start | bytes 3076
  47.0 122.9 %copy-start.32 = (f32[4,64]{1,0:T(4,128)}, f32[4,64]{1,0:T(4,128)S(1)}, u32[]{:S(2)}) copy-start(f32[4,64]{1,0:T(4,128)S(1)} %add.317) | copy-start | bytes 3076
  61.6 175.1 %reduce-scatter.13.cloned.1.call-start = ((), (), s32[]{:S(2)}) async-start(), calls=%async_computation.18 | async-start | bytes 5898240 | tf_op jit(solution)/shard_map/reduce_scatter | solution.py:38
  133.7 190.9 %reduce-scatter.17.cloned.1.call-start = ((), (), s32[]{:S(2)}) async-start(), calls=%async_computation.24 | async-start | bytes 5898240 | tf_op jit(solution)/shard_map/reduce_scatter | solution.py:38
  184.3 140.3 %copy-start.4 = (bf16[576,1024]{1,0:T(8,128)(2,1)S(1)}, bf16[576,1024]{1,0:T(8,128)(2,1)}, u32[]{:S(2)}) copy-start(bf16[576,1024]{1,0:T(8,128)(2,1)} %copy-done.3) | copy-start | bytes 3538948
  184.4 170.9 %all-gather.18.cloned.1.call-start = ((), (), s32[]{:S(2)}) async-start(), calls=%async_computation.20 | async-start | bytes 2359296 | tf_op jit(solution)/shard_map/all_gather | solution.py:123
  184.9 222.5 %all-gather.24.cloned.1.call-start = ((), (), s32[]{:S(2)}) async-start(), calls=%async_computation.25 | async-start | bytes 2949120 | tf_op jit(solution)/shard_map/all_gather | solution.py:21
  329.2 107.6 %all-gather.20.cloned.1.call-start = ((), (), s32[]{:S(2)}) async-start(), calls=%async_computation.21 | async-start | bytes 2359296 | tf_op jit(solution)/shard_map/all_gather | solution.py:124
  329.9 159.1 %all-gather.16.cloned.1.call-start = ((), (), s32[]{:S(2)}) async-start(), calls=%async_computation.19 | async-start | bytes 2949120 | tf_op jit(solution)/shard_map/all_gather | solution.py:21
  330.7 244.6 %reduce-scatter.19.cloned.1.call-start = ((), (), s32[]{:S(2)}) async-start(), calls=%async_computation.26 | async-start | bytes 5898240 | tf_op jit(solution)/shard_map/reduce_scatter | solution.py:25
  444.0 219.5 %reduce-scatter.15.cloned.1.call-start = ((), (), s32[]{:S(2)}) async-start(), calls=%async_computation.22 | async-start | bytes 5898240 | tf_op jit(solution)/shard_map/reduce_scatter | solution.py:25
  518.3 17.7 %all-to-all-start.2 = ((bf16[8,72,1024]{2,1,0:T(8,128)(2,1)}), bf16[8,72,1024]{2,1,0:T(8,128)(2,1)S(1)}, u32[]{:S(2)}, u32[]{:S(2)}) async-start(bf16[8,72,1024]{2,1,0:T(8,128)(2,1)} %bitcast.150), calls=%async_computation.6 | async-start | bytes 2359296 | tf_op jit(solution)/shard_map/all_to_all | solution.py:92
  522.6 202.3 %all-gather.30.cloned.1.call-start = ((), (), s32[]{:S(2)}) async-start(), calls=%async_computation.31 | async-start | bytes 2949120 | tf_op jit(solution)/shard_map/all_gather | solution.py:29
  673.9 102.0 %all-gather.26.cloned.1.call-start = ((), (), s32[]{:S(2)}) async-start(), calls=%async_computation.27 | async-start | bytes 2949120 | tf_op jit(solution)/shard_map/all_gather | solution.py:29
  678.1 184.1 %reduce-scatter.25.cloned.1.call-start = ((), (), s32[]{:S(2)}) async-start(), calls=%async_computation.32 | async-start | bytes 5898240 | tf_op jit(solution)/shard_map/reduce_scatter | solution.py:33
  740.6 209.6 %reduce-scatter.21.cloned.1.call-start = ((), (), s32[]{:S(2)}) async-start(), calls=%async_computation.28 | async-start | bytes 5898240 | tf_op jit(solution)/shard_map/reduce_scatter | solution.py:33
  791.4 219.6 %all-gather.28.cloned.1.call-start = ((), (), s32[]{:S(2)}) async-start(), calls=%async_computation.29 | async-start | bytes 2949120 | tf_op jit(solution)/shard_map/all_gather | solution.py:29
  958.4 52.7 %copy-start.19 = (bf16[256,1024]{1,0:T(8,128)(2,1)S(1)}, bf16[256,1024]{1,0:T(8,128)(2,1)}, u32[]{:S(2)}) copy-start(bf16[256,1024]{1,0:T(8,128)(2,1)} %all_gather.50) | copy-start | bytes 1572868
  960.0 146.8 %all-gather.32.cloned.1.call-start = ((), (), s32[]{:S(2)}) async-start(), calls=%async_computation.33 | async-start | bytes 2949120 | tf_op jit(solution)/shard_map/all_gather | solution.py:29
  961.7 51.9 %copy-start.38 = (f32[4,1152]{1,0:T(4,128)S(1)}, f32[4,1152]{1,0:T(4,128)}, u32[]{:S(2)}) copy-start(f32[4,1152]{1,0:T(4,128)} %copy-done.37) | copy-start | bytes 55300
  961.7 292.9 %reduce-scatter.23.cloned.1.call-start = ((), (), s32[]{:S(2)}) async-start(), calls=%async_computation.30 | async-start | bytes 5898240 | tf_op jit(solution)/shard_map/reduce_scatter | solution.py:33
  1106.8 184.8 %reduce-scatter.27.cloned.1.call-start = ((), (), s32[]{:S(2)}) async-start(), calls=%async_computation.34 | async-start | bytes 5898240 | tf_op jit(solution)/shard_map/reduce_scatter | solution.py:33
  1207.5 152.4 %reduce-scatter.29.cloned.1.call-start = ((), (), s32[]{:S(2)}) async-start(), calls=%async_computation.35 | async-start | bytes 3538944 | tf_op jit(solution)/shard_map/reduce_scatter | solution.py:258
  1216.1 184.9 %reduce-scatter.35.cloned.1.call-start = ((), (), s32[]{:S(2)}) async-start(), calls=%async_computation.38 | async-start | bytes 4718592 | tf_op jit(solution)/shard_map/reduce_scatter | solution.py:261
  1226.3 229.9 %reduce-scatter.33.cloned.1.call-start = ((), (), s32[]{:S(2)}) async-start(), calls=%async_computation.37 | async-start | bytes 4718592 | tf_op jit(solution)/shard_map/reduce_scatter | solution.py:260
  1245.4 57.6 %all-to-all-start.1 = ((bf16[8,72,1024]{2,1,0:T(8,128)(2,1)}), bf16[8,72,1024]{2,1,0:T(8,128)(2,1)S(1)}, u32[]{:S(2)}, u32[]{:S(2)}) async-start(bf16[8,72,1024]{2,1,0:T(8,128)(2,1)} %bitcast.149), calls=%async_computation.5 | async-start | bytes 2359296 | tf_op jit(solution)/shard_map/all_to_all | solution.py:248
  1249.9 246.3 %reduce-scatter.31.cloned.1.call-start = ((), (), s32[]{:S(2)}) async-start(), calls=%async_computation.36 | async-start | bytes 1179648 | tf_op jit(solution)/shard_map/reduce_scatter | solution.py:259
  1303.0 58.8 %all-to-all-start.3 = ((bf16[8,72,1024]{2,1,0:T(8,128)(2,1)}), bf16[8,72,1024]{2,1,0:T(8,128)(2,1)S(1)}, u32[]{:S(2)}, u32[]{:S(2)}) async-start(bf16[8,72,1024]{2,1,0:T(8,128)(2,1)} %bitcast.148), calls=%async_computation.11 | async-start | bytes 2359296 | tf_op jit(solution)/shard_map/all_to_all | solution.py:251
  (85 other events, 641.5 us)
Sparse Core Ops, SparseCore 0:
  10.5 33.0 all-gather.13
  46.8 52.6 all-gather.11
  101.0 49.2 all-gather.21
  152.5 84.1 reduce-scatter.12
  238.8 85.7 reduce-scatter.16
  326.4 28.7 all-gather.17
  357.4 50.0 all-gather.23
  409.3 27.4 all-gather.19
  439.0 50.0 all-gather.15
  491.2 84.1 reduce-scatter.18
  577.7 85.7 reduce-scatter.14
  674.0 50.9 all-gather.29
  726.5 49.2 all-gather.25
  778.0 84.1 reduce-scatter.24
  864.3 85.7 reduce-scatter.20
  960.1 50.9 all-gather.27
  1012.5 49.2 all-gather.31
  1106.9 83.9 reduce-scatter.22
  1207.6 83.9 reduce-scatter.26
  1294.8 50.4 reduce-scatter.28
  1349.6 51.2 reduce-scatter.34
  1404.9 51.2 reduce-scatter.32
  1460.3 35.9 reduce-scatter.30
where the time goes:
time: 1510 us; the launch traced here: 1500 us
  waiting for transfers between devices  933 us (62%)
  matrix products  340 us (23%)
  other arithmetic  66.8 us (4%)
  local copies, waits for them, and re-layouts  64.7 us (4%)
  blocking collectives  61.5 us (4%)
  starting transfers between devices  21.2 us (1%)
  between operations  15.5 us (1%)
    reduce_scatter x4, waiting for transfers between devices, collect_grads(): lax.psum_scatter(partial_rows, 'tensor', scatter_dimension=0, tiled=True)  193 us
    all_gather x4, waiting for transfers between devices, spread_rows(): return lax.all_gather(rows_local, 'tensor', axis=0, tiled=True)  150 us
    reduce_scatter x2, waiting for transfers between devices, attention_projection(): return lax.psum_scatter(out_part, 'tensor', scatter_dimension=0, tiled=True)  139 us
    all_gather x4, waiting for transfers between devices, spread_grads(): return lax.all_gather(rows_local, 'tensor', axis=0, tiled=True)  131 us
    reduce_scatter x2, waiting for transfers between devices, collect_feed(): lax.psum_scatter(partial_rows, 'tensor', scatter_dimension=0, tiled=True)  124 us
    dot_general x2, matrix products, on_device(): jnp.einsum('hqk,khd->qhd', score_back, key_rows, preferred_element_type=f...  64.2 us
    dot_general x2, matrix products, on_device(): jnp.einsum('hqk,qhd->khd', score_back, queries, preferred_element_type=fl...  63.3 us
    reduce_scatter x1, waiting for transfers between devices, on_device(): lax.psum_scatter(acc_up, 'dp', scatter_dimension=0, tiled=True)  55.3 us
  transfers between devices with their start and end apart: 27, of which 21 were waited for; matrix products, arithmetic and copies ran while one was open for 29% of the time, Pallas kernels for 0%

commit v1 on v0

v1 whole, which is shorter than its diff:
```python
import jax
import jax.numpy as jnp
from jax import lax
from jax.sharding import Mesh, PartitionSpec as P

DH = 64
MB = 2
F32 = jnp.float32
BF16 = jnp.bfloat16
ALL = ("chip", "core", "tensor")


def shift(x, step):
    n = lax.axis_size("tensor")
    return lax.ppermute(x, "tensor", [(i, (i + step) % n) for i in range(n)])


def flip(x, bit):
    n = lax.axis_size("chip")
    return lax.ppermute(x, "chip", [(i, i ^ bit) for i in range(n)])


def swap(x):
    return lax.ppermute(x, "core", [(0, 1), (1, 0)])


def chip_bits():
    n = lax.axis_size("chip")
    return [1 << i for i in range(n.bit_length() - 1)]


def pick(flag, x, y):
    return jnp.where(flag, x, y)


def ordered(core, mine, theirs, axis):
    return pick(
        core == 0,
        jnp.concatenate([mine, theirs], axis),
        jnp.concatenate([theirs, mine], axis),
    )


def relative(x, axis):
    chip = lax.axis_index("chip")
    n = lax.axis_size("chip")
    depth = x.shape[axis] // n
    for bit in chip_bits():
        parts = [lax.slice_in_dim(x, p * depth, (p + 1) * depth, axis=axis) for p in range(n)]
        other = jnp.concatenate([parts[p ^ bit] for p in range(n)], axis)
        x = pick((chip & bit) != 0, other, x)
    return x


def to_piece(shard, core):
    half = shard.shape[-1] // 2
    keep = lax.dynamic_slice_in_dim(shard, core * half, half, axis=1)
    give = lax.dynamic_slice_in_dim(shard, (1 - core) * half, half, axis=1)
    return ordered(core, keep, swap(give), 0)


def from_piece(piece, core):
    depth = piece.shape[0] // 2
    keep = lax.dynamic_slice_in_dim(piece, core * depth, depth, axis=0)
    give = lax.dynamic_slice_in_dim(piece, (1 - core) * depth, depth, axis=0)
    return ordered(core, keep, swap(give), 1)


def gather_line(piece):
    half = piece.shape[0] // 2
    below = shift(piece, 1)
    above = shift(piece, -1)
    far = jnp.concatenate([shift(below[:half], 1), shift(above[half:], -1)], 0)
    return piece, below, above, far


def gather_chips(unit, bits):
    depth = unit.shape[0]
    order = [0]
    for bit in bits:
        unit = jnp.concatenate([unit, flip(unit, bit)], 0)
        order = order + [p ^ bit for p in order]
    if order == sorted(order):
        return unit
    place = {p: i for i, p in enumerate(order)}
    return jnp.concatenate(
        [unit[place[p] * depth : (place[p] + 1) * depth] for p in range(len(order))], 0
    )


def gather_weight(piece):
    own, below, above, far = gather_line(piece)
    bits = chip_bits()
    return (
        gather_chips(jnp.concatenate([own, below], 1), bits),
        gather_chips(jnp.concatenate([above, far], 1), bits[::-1]),
    )


def scatter_chips(grad, bits):
    n = lax.axis_size("chip")
    depth = grad.shape[0] // n
    blocks = [grad[p * depth : (p + 1) * depth] for p in range(n)]
    names = list(range(n))
    for bit in bits:
        keep = [i for i, p in enumerate(names) if not p & bit]
        give = [names.index(names[i] ^ bit) for i in keep]
        there = flip(jnp.concatenate([blocks[i] for i in give], 0).astype(BF16), bit)
        blocks = [
            blocks[i] + there[j * depth : (j + 1) * depth].astype(F32) for j, i in enumerate(keep)
        ]
        names = [names[i] for i in keep]
    return blocks[0]


def scatter_line(own, below, above, far):
    half = own.shape[0] // 2
    low = far.astype(BF16)
    first = shift(low[:half], 1)
    second = shift(low[half:], -1)
    above = jnp.concatenate([above[:half] + first.astype(F32), above[half:]], 0).astype(BF16)
    below = jnp.concatenate([below[:half], below[half:] + second.astype(F32)], 0).astype(BF16)
    return own + shift(above, 1).astype(F32) + shift(below, -1).astype(F32)


def scatter_grad(grad_a, grad_b, core):
    bits = chip_bits()
    got_a = scatter_chips(grad_a, bits[::-1])
    got_b = scatter_chips(grad_b, bits)
    half = got_a.shape[1] // 2
    piece = scatter_line(got_a[:, :half], got_a[:, half:], got_b[:, :half], got_b[:, half:])
    return from_piece(piece, core)


def exchange_sum(make_part, own_rows):
    there = swap(make_part(True))
    return make_part(False) + there


def inverse_of(slots):
    count = slots.shape[0]
    marks = jnp.arange(count, dtype=jnp.int32)
    hit = slots[None, :] == marks[:, None]
    return jnp.sum(jnp.where(hit, marks[None, :], 0), axis=1)


def normalize(values):
    center = values - jnp.mean(values, axis=-1, keepdims=True)
    spread = jnp.mean(center * center, axis=-1, keepdims=True)
    inverse = lax.rsqrt(spread + 1e-05)
    return center * inverse, inverse


def norm_back(grad, normed, inverse, gain):
    scaled = grad * gain
    mean_one = jnp.mean(scaled, axis=-1, keepdims=True)
    mean_two = jnp.mean(scaled * normed, axis=-1, keepdims=True)
    return inverse * (scaled - mean_one - normed * mean_two)


def nn(x, y):
    return jnp.dot(x, y, preferred_element_type=F32)


def nt(x, y):
    return lax.dot_general(x, y, (((1,), (1,)), ((), ())), preferred_element_type=F32)


def tn(x, y):
    return lax.dot_general(x, y, (((0,), (0,)), ((), ())), preferred_element_type=F32)


def gelu_both(z):
    gate = 0.5 * (1.0 + lax.erf(z * 0.7071067811865476))
    slope = gate + z * jnp.exp(-0.5 * z * z) * 0.3989422804014327
    return z * gate, slope


def masked_scores(queries, key_rows, allowed, scale):
    raw = jnp.einsum("qhd,khd->hqk", queries, key_rows, preferred_element_type=F32) * scale
    return jnp.where(allowed[None], raw, -1e30)


def on_device(
    tokens,
    cotangent,
    deal,
    source,
    lengths,
    qkv_weight,
    query_bias,
    value_bias,
    out_weight,
    out_bias,
    first_gain,
    first_shift,
    up_weight,
    up_bias,
    down_weight,
    down_bias,
    second_gain,
    second_shift,
):
    core = lax.axis_index("core")
    line = lax.axis_index("tensor")
    split_ways = lax.axis_size("tensor")
    chips = lax.axis_size("chip")
    data_ways = 2 * chips
    rows, width = tokens.shape
    per_peer = rows // data_ways
    group_rows = split_ways * rows
    quarter = rows // MB
    local_width = qkv_weight.shape[2]
    local_hidden = up_weight.shape[1]
    scale = DH ** (-0.5)
    dp = ("chip", "core")

    targets = deal // group_rows
    one_hot = (targets[:, None] == jnp.arange(data_ways, dtype=jnp.int32)[None, :]).astype(
        jnp.int32
    )
    send_slot = targets * per_peer + jnp.sum(one_hot * jnp.cumsum(one_hot, axis=0), axis=1) - 1
    senders = source // group_rows
    earlier = (senders[:, None] == senders[None, :]) & (source[None, :] < source[:, None])
    recv_slot = senders * per_peer + jnp.sum(earlier.astype(jnp.int32), axis=1)
    odd = line % 2
    first_rows = lax.dynamic_slice_in_dim(recv_slot, odd * quarter, quarter)
    second_rows = lax.dynamic_slice_in_dim(recv_slot, (1 - odd) * quarter, quarter)
    recv_order = jnp.concatenate([first_rows, second_rows])
    send_order = inverse_of(send_slot)
    back_order = inverse_of(recv_order)

    def moves(which):
        pairs = []
        for k in range(2):
            for t in range(split_ways):
                m = t % 2 if which == 0 else 1 - t % 2
                pairs.append((k * split_ways + t, (t // 2) * split_ways + 2 * k + m))
        return pairs

    def to_owner(x):
        outgoing = x[send_order]
        arrived = lax.all_to_all(outgoing, dp, split_axis=0, concat_axis=0, tiled=True)
        work = relative(arrived[recv_order], 1)
        return jnp.concatenate(
            [
                lax.ppermute(work[:quarter], ("core", "tensor"), moves(0)),
                lax.ppermute(work[quarter:], ("core", "tensor"), moves(1)),
            ],
            0,
        )

    def from_owner(x):
        back = [[(b, a) for a, b in moves(which)] for which in range(2)]
        work = jnp.concatenate(
            [
                lax.ppermute(x[:quarter], ("core", "tensor"), back[0]),
                lax.ppermute(x[quarter:], ("core", "tensor"), back[1]),
            ],
            0,
        )
        outgoing = relative(work, 1)[back_order]
        arrived = lax.all_to_all(outgoing, dp, split_axis=0, concat_axis=0, tiled=True)
        return arrived[send_slot]

    rows_x = to_owner(tokens)

    which_group = line // 2
    lengths_here = pick(core == which_group, lengths[0], swap(lengths[0]))
    seq_ends = jnp.cumsum(lax.dynamic_index_in_dim(lengths_here, odd, 0, keepdims=False))
    steps = jnp.arange(quarter, dtype=jnp.int32)
    positions = jnp.concatenate(
        [
            (2 * c + b) * quarter + steps
            for c in (core, 1 - core)
            for b in (odd, 1 - odd)
        ]
    )
    seq_ids = jnp.sum((positions[:, None] >= seq_ends[None, :]).astype(jnp.int32), axis=1)
    allowed = seq_ids[:, None] == seq_ids[None, :]

    depth = qkv_weight.shape[1]
    qkv_pieces = [to_piece(qkv_weight[i], core) for i in range(3)]
    qkv_a, qkv_b = gather_weight(jnp.concatenate(qkv_pieces, 1))
    out_a, out_b = gather_weight(to_piece(out_weight.T, core))
    up_a, up_b = gather_weight(to_piece(up_weight, core))
    down_a, down_b = gather_weight(to_piece(down_weight.T, core))
    qkv_w = jnp.concatenate([qkv_a, qkv_b], 1)
    out_w = jnp.concatenate([out_a, out_b], 1)

    positions_on_line = [(line + step) % split_ways for step in (0, -1, 1, 2)]

    def bias_units(vector, unit):
        half = unit // 2
        return [
            lax.dynamic_slice_in_dim(vector, where * unit + core * half, half)
            for where in positions_on_line
        ]

    def place_units(parts, unit):
        half = unit // 2
        out = jnp.zeros((unit * split_ways,), F32)
        for where, part in zip(positions_on_line, parts):
            out = lax.dynamic_update_slice_in_dim(out, part, where * unit + core * half, 0)
        return out

    query_units = bias_units(query_bias.astype(F32), local_width)
    value_units = bias_units(value_bias.astype(F32), local_width)
    up_local = jnp.concatenate(bias_units(up_bias.astype(F32), local_hidden))
    zero_unit = jnp.zeros_like(query_units[0])
    qkv_bias = jnp.concatenate(
        [part for q, v in zip(query_units, value_units) for part in (q, zero_unit, v)]
    )
    out_bias_f, first_gain_f, first_shift_f, down_bias_f, second_gain_f, second_shift_f = (
        relative(v.astype(F32), 0)
        for v in (out_bias, first_gain, first_shift, down_bias, second_gain, second_shift)
    )

    pair_x = jnp.concatenate([rows_x, swap(rows_x)], 0)
    projected = (nn(pair_x, qkv_w) + qkv_bias).astype(BF16)
    unit = local_width // 2
    count = projected.shape[0]
    heads = split_ways * unit // DH

    def heads_of(which):
        parts = [
            projected[:, (3 * u + which) * unit : (3 * u + which + 1) * unit]
            for u in range(split_ways)
        ]
        return jnp.concatenate(parts, 1).reshape(count, heads, DH)

    queries, key_rows, value_rows = heads_of(0), heads_of(1), heads_of(2)
    scores = masked_scores(queries, key_rows, allowed, scale)
    row_max = jnp.max(scores, axis=-1, keepdims=True)
    log_total = row_max + jnp.log(jnp.sum(jnp.exp(scores - row_max), axis=-1, keepdims=True))
    probs_low = jnp.exp(scores - log_total).astype(BF16)
    mixed = (
        jnp.einsum("hqk,khd->qhd", probs_low, value_rows, preferred_element_type=F32)
        .astype(BF16)
        .reshape(count, heads * DH)
    )
    first_sum = rows_x.astype(F32) + exchange_sum(
        lambda other: nt(mixed[rows:] if other else mixed[:rows], out_w), rows
    ) + out_bias_f
    first_normed, first_inverse = normalize(first_sum)
    first_out = first_normed * first_gain_f + first_shift_f
    first_low = first_out.astype(BF16)
    pair_y = jnp.concatenate([first_low, swap(first_low)], 0)
    hidden, slope = [], []
    half_hidden = up_a.shape[1]
    for i, w in enumerate((up_a, up_b)):
        z = nn(pair_y, w) + up_local[i * half_hidden : (i + 1) * half_hidden]
        u, s = gelu_both(z)
        hidden.append(u.astype(BF16))
        slope.append(s)

    def down_part(other):
        where = slice(rows, None) if other else slice(0, rows)
        return nt(hidden[0][where], down_a) + nt(hidden[1][where], down_b)

    second_sum = first_out + exchange_sum(down_part, rows) + down_bias_f
    second_normed, second_inverse = normalize(second_sum)
    result = (second_normed * second_gain_f + second_shift_f).astype(BF16)

    rows_g = to_owner(cotangent).astype(F32)
    second_back = norm_back(rows_g, second_normed, second_inverse, second_gain_f)
    second_gain_grad = jnp.sum(rows_g * second_normed, axis=0)
    second_shift_grad = jnp.sum(rows_g, axis=0)
    down_bias_grad = jnp.sum(second_back, axis=0)
    second_low = second_back.astype(BF16)
    pair_m = jnp.concatenate([second_low, swap(second_low)], 0)
    down_grad_t = scatter_grad(tn(pair_m, hidden[0]), tn(pair_m, hidden[1]), core)
    pre_low, up_bias_parts = [], []
    for w, s in zip((down_a, down_b), slope):
        pre = nn(pair_m, w) * s
        up_bias_parts.append(jnp.sum(pre, axis=0))
        pre_low.append(pre.astype(BF16))
    up_grad = scatter_grad(tn(pair_y, pre_low[0]), tn(pair_y, pre_low[1]), core)

    def up_part(other):
        where = slice(rows, None) if other else slice(0, rows)
        return nt(pre_low[0][where], up_a) + nt(pre_low[1][where], up_b)

    first_grad = second_back + exchange_sum(up_part, rows)
    first_back = norm_back(first_grad, first_normed, first_inverse, first_gain_f)
    first_gain_grad = jnp.sum(first_grad * first_normed, axis=0)
    first_shift_grad = jnp.sum(first_grad, axis=0)
    out_bias_grad = jnp.sum(first_back, axis=0)
    first_back_low = first_back.astype(BF16)
    pair_o = jnp.concatenate([first_back_low, swap(first_back_low)], 0)
    out_half = out_a.shape[1]
    out_grad = tn(pair_o, mixed)
    out_grad_t = scatter_grad(out_grad[:, :out_half], out_grad[:, out_half:], core)
    mixed_back = nn(pair_o, out_w).astype(BF16).reshape(count, heads, DH)
    value_back = jnp.einsum(
        "hqk,qhd->khd", probs_low, mixed_back, preferred_element_type=F32
    ).reshape(count, heads * DH)
    prob_back = jnp.einsum(
        "qhd,khd->hqk", mixed_back, value_rows, preferred_element_type=F32
    )
    again = masked_scores(queries, key_rows, allowed, scale)
    probs = jnp.exp(again - log_total)
    row_dot = jnp.sum(prob_back * probs, axis=-1, keepdims=True)
    score_back = (probs * (prob_back - row_dot) * scale).astype(BF16)
    query_back = jnp.einsum(
        "hqk,khd->qhd", score_back, key_rows, preferred_element_type=F32
    ).reshape(count, heads * DH)
    key_back = jnp.einsum(
        "hqk,qhd->khd", score_back, queries, preferred_element_type=F32
    ).reshape(count, heads * DH)
    query_bias_local = jnp.sum(query_back, axis=0)
    value_bias_local = jnp.sum(value_back, axis=0)
    back_parts = []
    for u in range(split_ways):
        for part in (query_back, key_back, value_back):
            back_parts.append(part[:, u * unit : (u + 1) * unit].astype(BF16))
    proj_back = jnp.concatenate(back_parts, 1)
    qkv_half = qkv_a.shape[1]
    qkv_grad_w = tn(pair_x, proj_back)
    qkv_piece = scatter_grad_piece(qkv_grad_w[:, :qkv_half], qkv_grad_w[:, qkv_half:])
    qkv_grad = jnp.stack(
        [from_piece(qkv_piece[:, i * unit : (i + 1) * unit], core) for i in range(3)]
    )
    input_back = first_back + exchange_sum(
        lambda other: nt(proj_back[rows:] if other else proj_back[:rows], qkv_w), rows
    )

    layer_out = from_owner(result)
    tokens_grad = from_owner(input_back.astype(BF16)).astype(F32)

    units = lambda v, n: [v[i * n : (i + 1) * n] for i in range(split_ways)]
    feature = [
        relative(v, 0)
        for v in (
            out_bias_grad,
            first_gain_grad,
            first_shift_grad,
            down_bias_grad,
            second_gain_grad,
            second_shift_grad,
        )
    ]
    placed = [
        place_units(units(query_bias_local, unit), local_width),
        place_units(units(value_bias_local, unit), local_width),
        place_units(units(jnp.concatenate(up_bias_parts), local_hidden // 2), local_hidden),
    ]
    packed = jnp.concatenate(feature + placed).reshape(-1, 128)
    packed = packed + swap(packed)
    for bit in chip_bits():
        packed = packed + flip(packed, bit)
    step = 1
    while step < split_ways:
        packed = packed + lax.ppermute(
            packed, "tensor", [(i, i ^ step) for i in range(split_ways)]
        )
        step *= 2
    packed = packed.reshape(-1)
    sizes = [v.shape[0] for v in feature + placed]
    ends = [sum(sizes[: i + 1]) for i in range(len(sizes))]
    (
        out_bias_grad,
        first_gain_grad,
        first_shift_grad,
        down_bias_grad,
        second_gain_grad,
        second_shift_grad,
        query_bias_grad,
        value_bias_grad,
        up_bias_grad,
    ) = (packed[end - size : end] for end, size in zip(ends, sizes))
    return (
        layer_out,
        tokens_grad,
        qkv_grad,
        query_bias_grad,
        value_bias_grad,
        out_grad_t.T,
        out_bias_grad,
        first_gain_grad,
        first_shift_grad,
        up_grad,
        up_bias_grad,
        down_grad_t.T,
        down_bias_grad,
        second_gain_grad,
        second_shift_grad,
    )


def scatter_grad_piece(grad_a, grad_b):
    bits = chip_bits()
    got_a = scatter_chips(grad_a, bits[::-1])
    got_b = scatter_chips(grad_b, bits)
    half = got_a.shape[1] // 2
    return scatter_line(got_a[:, :half], got_a[:, half:], got_b[:, :half], got_b[:, half:])


def solution(mesh):
    data_ways, split_ways = mesh.shape["dp"], mesh.shape["tensor"]
    fine = Mesh(mesh.devices.reshape(data_ways // 2, 2, split_ways), ALL)
    dp = ("chip", "core")
    in_specs = (
        P(ALL, None),
        P(ALL, None),
        P(ALL),
        P(ALL),
        P(dp, None, None),
        P(None, dp, "tensor"),
        P(),
        P(),
        P("tensor", dp),
        P(),
        P(),
        P(),
        P(dp, "tensor"),
        P(),
        P("tensor", dp),
        P(),
        P(),
        P(),
    )
    out_specs = (
        P(ALL, None),
        P(ALL, None),
        P(None, dp, "tensor"),
        P(),
        P(),
        P("tensor", dp),
        P(),
        P(),
        P(),
        P(dp, "tensor"),
        P(),
        P("tensor", dp),
        P(),
        P(),
        P(),
    )
    return jax.shard_map(
        on_device, mesh=fine, in_specs=in_specs, out_specs=out_specs, check_vma=False
    )
```

time: 1510 us -> 877 us (0.58)
  waiting for transfers between devices: 933 us -> 187 us
  starting transfers between devices: 21.2 us -> 182 us
  blocking collectives: 61.5 us -> 0 us
  matrix products: 340 us -> 300 us
  other arithmetic: 66.8 us -> 98.8 us
  local copies, waits for them, and re-layouts: 64.7 us -> 89.5 us
    reduce_scatter x12 -> x0, waiting for transfers between devices: 586 us -> none  [the longest x4 193 us: collect_grads(): lax.psum_scatter(partial_rows, 'tensor', scatter_dimension=0, tiled=True)]
    all_gather x11 -> x0, waiting for transfers between devices: 318 us -> none  [the longest x4 150 us: spread_rows(): return lax.all_gather(rows_local, 'tensor', axis=0, tiled=True)]
    ppermute x0 -> x98, waiting for transfers between devices: none -> 177 us  [the longest x34 79.5 us: flip(): return lax.ppermute(x, 'chip', [(i, i ^ bit) for i in range(n)])]
    ppermute x0 -> x98, starting transfers between devices: none -> 158 us  [the longest x32 69.1 us: shift(): return lax.ppermute(x, 'tensor', [(i, (i + step) % n) for i in range(n)])]
    psum x1 -> x0, blocking collectives: 48.1 us -> none  [on_device(): lax.psum((query_placed, value_placed, acc_out_bias, acc_first_gain, acc_f...]
    concatenate x0 -> x36, other arithmetic: none -> 40.6 us  [the longest x1 20.9 us: on_device(): qkv_w = jnp.concatenate([qkv_a, qkv_b], 1)]
    dot_general x30 -> x27, matrix products: 275 us -> 251 us  [the longest x1 67.2 us: on_device(): jnp.einsum('hqk,qhd->khd', score_back, queries, preferred_element_type=F32)]
    slice x7 -> x78, local copies, waits for them, and re-layouts: 6.25 us -> 25.9 us  [the longest x10 8.74 us: on_device(): units = lambda v, n: [v[i * n:(i + 1) * n] for i in range(split_ways)]]
  transfers between devices with their start and end apart: 27 -> 102, of which waited for: 21 -> 38; matrix products, arithmetic and copies ran while one was open for 29% -> 33% of each run, Pallas kernels for 0% -> 0%
where the time goes in v1:
time: 877 us; the launch traced here: 861 us
  matrix products  300 us (34%)
  waiting for transfers between devices  187 us (21%)
  starting transfers between devices  182 us (21%)
  other arithmetic  98.8 us (11%)
  local copies, waits for them, and re-layouts  89.5 us (10%)
    ppermute x34, waiting for transfers between devices, flip(): return lax.ppermute(x, 'chip', [(i, i ^ bit) for i in range(n)])  79.5 us
    ppermute x32, starting transfers between devices, shift(): return lax.ppermute(x, 'tensor', [(i, (i + step) % n) for i in range(n)])  69.1 us
    dot_general x1, matrix products, on_device(): jnp.einsum('hqk,qhd->khd', score_back, queries, preferred_element_type=F32)  67.2 us
    dot_general x1, matrix products, on_device(): jnp.einsum('hqk,khd->qhd', score_back, key_rows, preferred_element_type=F32)  65.1 us
    ppermute x2, waiting for transfers between devices, from_owner(): lax.ppermute(x[:quarter], ('core', 'tensor'), back[0])  38 us
    dot_general x12, matrix products, nt(): lax.dot_general(x, y, (((1,), (1,)), ((), ())), preferred_element_type=F32)  36.5 us
    dot_general x6, matrix products, nn(): return jnp.dot(x, y, preferred_element_type=F32)  35.8 us
    ppermute x32, waiting for transfers between devices, shift(): return lax.ppermute(x, 'tensor', [(i, (i + step) % n) for i in range(n)])  34.8 us
  transfers between devices with their start and end apart: 102, of which 38 were waited for; matrix products, arithmetic and copies ran while one was open for 33% of the time, Pallas kernels for 0%

profile of v1, /device:TPU:1, one launch (start us, length us, event | category | flops | bytes accessed | tf_op | source)
XLA Modules:
  0.0 861.3 jit_solution(2463099064358121798)
XLA Ops:
  10.7 5.4 all-to-all-start
  62.0 10.3 %all-to-all-start.2 = ((bf16[8,72,1024]{2,1,0:T(8,128)(2,1)}), bf16[8,72,1024]{2,1,0:T(8,128)(2,1)S(1)}, u32[]{:S(2)}, u32[]{:S(2)}) async-start(bf16[8,72,1024]{2,1,0:T(8,128)(2,1)} %bitcast.27), calls=%async_computation.2 | async-start | bytes 2359296 | tf_op jit(solution)/shard_map/all_to_all | solution.py:243
  84.5 6.2 collective-permute-start.30
  95.7 5.6 collective-permute-done.1
  101.6 20.9 %maximum_maximum_fusion = bf16[1024,1536]{0,1:T(8,128)(2,1)S(1)} fusion(bf16[256,768]{0,1:T(8,128)(2,1)S(1)} %get-tuple-element.153, bf16[256,768]{0,1:T(8,128)(2,1)S(1)} %copy-done.45, bf16[256,768]{0,1:T(8,128)(2,1)S(1)} %get-tuple-element.152, bf16[128,384]{0,1:T(8,128)(2,1)S(1)} %copy-done.57, bf16[128,384]{0,1:T(8,128)(2,1)S(1)} %copy-done.55, ...), kind=kLoop, calls=%fused_computation.53 | loop fusion | flops 37748736 | bytes 6291456 | tf_op jit(solution)/shard_map/concatenate | solution.py:288
  134.6 17.3 %fusion.193 = (f32[8,1152]{1,0:T(8,128)S(1)}, f32[8,1152,1152]{1,2,0:T(8,128)}) fusion(bf16[1152,8,64]{0,2,1:T(8,128)(2,1)S(1)} %bitcast.125, bf16[1152,8,64]{0,2,1:T(8,128)(2,1)S(1)} %bitcast.123, pred[1152,1152]{0,1:T(8,128)(4,1)} %broadcast_compare_fusion), kind=kOutput, calls=%fused_computation.459 | convolution fusion | flops 1390795776 | bytes 46190592 | tf_op jit(solution)/shard_map/qhd,khd->hqk/dot_general | solution.py:180
  152.0 16.5 %exponential_reduce_fusion = f32[8,1152]{1,0:T(8,128)S(1)} fusion(f32[8,1152,1152]{1,2,0:T(8,128)} %get-tuple-element.299, f32[8,1152]{1,0:T(8,128)S(1)} %get-tuple-element.298), kind=kLoop, calls=%fused_computation.15 | loop fusion | flops 21224448 | bytes 42541056 | tf_op jit(solution)/shard_map/reduce_sum | solution.py:335
  170.4 16.3 %fusion.37 = bf16[8,64,1152]{2,1,0:T(8,128)(2,1)S(1)} fusion(bf16[1152,8,64]{0,2,1:T(8,128)(2,1)S(1)} %bitcast.113, f32[8,1152,1152]{1,2,0:T(8,128)} %get-tuple-element.299, f32[8,1152]{1,0:T(8,128)} %log_add_fusion), kind=kOutput, calls=%fused_computation.54 | convolution fusion | flops 1380777984 | bytes 44863488 | tf_op jit(solution)/shard_map/hqk,khd->qhd/dot_general | solution.py:338
  194.5 6.2 collective-permute-start.27
  246.5 7.7 collective-permute-done.42
  274.2 10.4 %collective-permute-done.38 = bf16[512,1024]{0,1:T(8,128)(2,1)} collective-permute-done((bf16[512,1024]{0,1:T(8,128)(2,1)}, bf16[512,1024]{0,1:T(8,128)(2,1)}, u32[]{:S(2)}, u32[]{:S(2)}) %collective-permute-start.38) | collective-permute-done | bytes 1048608 | tf_op jit(solution)/shard_map/ppermute | solution.py:20
  285.9 21.2 %collective-permute-done.43 = bf16[512,1024]{0,1:T(8,128)(2,1)} collective-permute-done((bf16[512,1024]{0,1:T(8,128)(2,1)}, bf16[512,1024]{0,1:T(8,128)(2,1)}, u32[]{:S(2)}, u32[]{:S(2)}) %collective-permute-start.43) | collective-permute-done | bytes 1048608 | tf_op jit(solution)/shard_map/ppermute | solution.py:20
  308.5 7.3 multiply_convert_fusion
  318.8 7.2 multiply_convert_fusion.1
  349.9 7.8 collective-permute-done.48
  363.0 9.6 %collective-permute-start.45 = (bf16[288,1024]{1,0:T(8,128)(2,1)S(1)}, bf16[288,1024]{1,0:T(8,128)(2,1)S(1)}, u32[]{:S(2)}, u32[]{:S(2)}) collective-permute-start(bf16[288,1024]{1,0:T(8,128)(2,1)S(1)} %get-tuple-element.135), channel_id=1, source_target_pairs={{0,0},{1,1},{4,2},{5,3},{2,4},{3,5},{6,6},{7,7},{8,8},{9,9},{12,10... | collective-permute-start | bytes 1769480 | tf_op jit(solution)/shard_map/ppermute | solution.py:257
  374.3 18.5 %collective-permute-done.45 = bf16[288,1024]{1,0:T(8,128)(2,1)S(1)} collective-permute-done((bf16[288,1024]{1,0:T(8,128)(2,1)S(1)}, bf16[288,1024]{1,0:T(8,128)(2,1)S(1)}, u32[]{:S(2)}, u32[]{:S(2)}) %collective-permute-start.45) | collective-permute-done | bytes 589856 | tf_op jit(solution)/shard_map/ppermute | solution.py:257
  414.9 5.7 fusion.133
  426.9 8.6 fusion.134
  465.7 9.7 %collective-permute-done.92 = bf16[256,1024]{0,1:T(8,128)(2,1)S(1)} collective-permute-done((bf16[256,1024]{0,1:T(8,128)(2,1)S(1)}, bf16[256,1024]{0,1:T(8,128)(2,1)S(1)}, u32[]{:S(2)}, u32[]{:S(2)}) %collective-permute-start.92) | collective-permute-done | bytes 524320 | tf_op jit(solution)/shard_map/ppermute | solution.py:20
  475.8 6.6 collective-permute-start.93
  487.0 6.6 collective-permute-start.84
  501.4 8.1 collective-permute-done.85
  515.2 5.7 collective-permute-start.88
  545.3 16.2 %fusion.137 = (f32[8,64]{1,0:T(8,128)S(1)}, bf16[1152,8,64]{0,2,1:T(8,128)(2,1)S(1)}) fusion(bf16[1152,8,64]{0,2,1:T(8,128)(2,1)S(1)} %bitcast.115, f32[8,1152,1152]{1,2,0:T(8,128)} %get-tuple-element.299, f32[8,1152]{1,0:T(8,128)S(1)} %copy-done.17), kind=kOutput, calls=%fused_computation.403 | convolution fusion | flops 1381367296 | bytes 44865536 | tf_op jit(solution)/shard_map/hqk,qhd->khd/dot_general | solution.py:395
  561.5 16.5 %fusion.201 = f32[8,1152,1152]{1,2,0:T(8,128)} fusion(bf16[1152,8,64]{0,2,1:T(8,128)(2,1)S(1)} %bitcast.116, bf16[1152,8,64]{0,2,1:T(8,128)(2,1)S(1)} %bitcast.114), kind=kOutput, calls=%fused_computation.465 | convolution fusion | flops 1358954496 | bytes 44826624 | tf_op jit(solution)/shard_map/qhd,khd->hqk/dot_general | solution.py:398
  578.0 65.1 %fusion.138 = (f32[8,64]{1,0:T(8,128)S(1)}, bf16[1152,8,64]{0,2,1:T(8,128)(2,1)}) fusion(bf16[1152,8,64]{0,2,1:T(8,128)(2,1)S(1)} %bitcast.124, f32[8,1152,1152]{1,2,0:T(8,128)} %fusion.201, f32[8,1152,1152]{1,2,0:T(8,128)} %get-tuple-element.299, f32[8,1152]{1,0:T(8,128)} %log_add_fusion), kind=kOutput, calls=%fused_computation.404 | convolution fusion | flops 1434461824 | bytes 87332864 | tf_op jit(solution)/shard_map/hqk,khd->qhd/dot_general | solution.py:405
  643.1 67.2 %fusion.40 = bf16[8,64,1152]{2,1,0:T(8,128)(2,1)} fusion(bf16[1152,8,64]{0,2,1:T(8,128)(2,1)} %bitcast.126, f32[8,1152,1152]{1,2,0:T(8,128)} %fusion.201, f32[8,1152,1152]{1,2,0:T(8,128)} %get-tuple-element.299, f32[8,1152]{1,0:T(8,128)} %log_add_fusion), kind=kOutput, calls=%fused_computation.56 | convolution fusion | flops 1433872512 | bytes 87330816 | tf_op jit(solution)/shard_map/hqk,qhd->khd/dot_general | solution.py:408
  766.3 12.9 %collective-permute-done.72 = bf16[256,256]{1,0:T(8,128)(2,1)S(1)} collective-permute-done((bf16[256,256]{1,0:T(8,128)(2,1)S(1)}, bf16[256,256]{1,0:T(8,128)(2,1)S(1)}, u32[]{:S(2)}, u32[]{:S(2)}) %collective-permute-start.72) | collective-permute-done | bytes 131104 | tf_op jit(solution)/shard_map/ppermute | solution.py:20
  785.9 6.2 collective-permute-done.58
  814.2 19.5 %collective-permute-done.53 = bf16[288,1024]{1,0:T(8,128)(2,1)S(1)} collective-permute-done((bf16[288,1024]{1,0:T(8,128)(2,1)}, bf16[288,1024]{1,0:T(8,128)(2,1)S(1)}, u32[]{:S(2)}, u32[]{:S(2)}) %collective-permute-start.53) | collective-permute-done | bytes 589856 | tf_op jit(solution)/shard_map/ppermute | solution.py:257
  846.0 10.5 %all-to-all-done.3 = bf16[8,72,1024]{2,1,0:T(8,128)(2,1)S(1)} async-done(((bf16[8,72,1024]{2,1,0:T(8,128)(2,1)}), bf16[8,72,1024]{2,1,0:T(8,128)(2,1)S(1)}, u32[]{:S(2)}, u32[]{:S(2)}) %all-to-all-start.3) | async-done | bytes 1179680 | tf_op jit(solution)/shard_map/all_to_all | solution.py:263
  (902 shorter events, 397.4 us)
Async XLA Ops:
  1.8 28.5 %collective-permute-start.4 = (bf16[128,128]{0,1:T(8,128)(2,1)S(1)}, bf16[128,128]{0,1:T(8,128)(2,1)S(1)}, u32[]{:S(2)}, u32[]{:S(2)}) collective-permute-start(bf16[128,128]{0,1:T(8,128)(2,1)S(1)} %bitcast.147), channel_id=1, source_target_pairs={{0,4},{4,0},{1,5},{5,1},{2,6},{6,2},{3,7},{7,3},{8,12},{12,8},{9,1... | collective-permute-start | bytes 98312 | tf_op jit(solution)/shard_map/ppermute | solution.py:24
  2.1 30.4 %collective-permute-start.5 = (bf16[128,128]{0,1:T(8,128)(2,1)S(1)}, bf16[128,128]{0,1:T(8,128)(2,1)S(1)}, u32[]{:S(2)}, u32[]{:S(2)}) collective-permute-start(bf16[128,128]{0,1:T(8,128)(2,1)S(1)} %bitcast.145), channel_id=1, source_target_pairs={{0,4},{4,0},{1,5},{5,1},{2,6},{6,2},{3,7},{7,3},{8,12},{12,8},{9,1... | collective-permute-start | bytes 98312 | tf_op jit(solution)/shard_map/ppermute | solution.py:24
  2.7 29.8 %collective-permute-start.3 = (bf16[128,128]{0,1:T(8,128)(2,1)S(1)}, bf16[128,128]{0,1:T(8,128)(2,1)S(1)}, u32[]{:S(2)}, u32[]{:S(2)}) collective-permute-start(bf16[128,128]{0,1:T(8,128)(2,1)S(1)} %bitcast.146), channel_id=1, source_target_pairs={{0,4},{4,0},{1,5},{5,1},{2,6},{6,2},{3,7},{7,3},{8,12},{12,8},{9,1... | collective-permute-start | bytes 98312 | tf_op jit(solution)/shard_map/ppermute | solution.py:24
  10.7 51.3 %all-to-all-start = ((bf16[8,72,1024]{2,1,0:T(8,128)(2,1)}), bf16[8,72,1024]{2,1,0:T(8,128)(2,1)S(1)}, u32[]{:S(2)}, u32[]{:S(2)}) async-start(bf16[8,72,1024]{2,1,0:T(8,128)(2,1)} %bitcast.4), calls=%async_computation | async-start | bytes 2359296 | tf_op jit(solution)/shard_map/all_to_all | solution.py:243
  28.6 164.9 %collective-permute-start.26 = (bf16[128,512]{0,1:T(8,128)(2,1)}, bf16[128,512]{0,1:T(8,128)(2,1)}, u32[]{:S(2)}, u32[]{:S(2)}) collective-permute-start(bf16[128,512]{0,1:T(8,128)(2,1)} %copy.118), channel_id=1, source_target_pairs={{0,4},{4,0},{1,5},{5,1},{2,6},{6,2},{3,7},{7,3},{8,12},{12,8},{9,1... | collective-permute-start | bytes 393224 | tf_op jit(solution)/shard_map/ppermute | solution.py:24
  59.1 42.5 %collective-permute-start.8 = (bf16[512,768]{0,1:T(8,128)(2,1)}, bf16[512,768]{0,1:T(8,128)(2,1)}, u32[]{:S(2)}, u32[]{:S(2)}) collective-permute-start(bf16[512,768]{0,1:T(8,128)(2,1)} %pad_maximum_fusion.19), channel_id=1, source_target_pairs={{0,16},{8,24},{16,0},{24,8},{1,17},{9,25},{17,1},{25,9},{2,18},{10... | collective-permute-start | bytes 2359304 | tf_op jit(solution)/shard_map/ppermute | solution.py:20
  62.0 209.0 %all-to-all-start.2 = ((bf16[8,72,1024]{2,1,0:T(8,128)(2,1)}), bf16[8,72,1024]{2,1,0:T(8,128)(2,1)S(1)}, u32[]{:S(2)}, u32[]{:S(2)}) async-start(bf16[8,72,1024]{2,1,0:T(8,128)(2,1)} %bitcast.27), calls=%async_computation.2 | async-start | bytes 2359296 | tf_op jit(solution)/shard_map/all_to_all | solution.py:243
  84.5 116.2 %collective-permute-start.30 = (bf16[128,512]{0,1:T(8,128)(2,1)}, bf16[128,512]{0,1:T(8,128)(2,1)}, u32[]{:S(2)}, u32[]{:S(2)}) collective-permute-start(bf16[128,512]{0,1:T(8,128)(2,1)} %get-tuple-element.175), channel_id=1, source_target_pairs={{0,4},{4,0},{1,5},{5,1},{2,6},{6,2},{3,7},{7,3},{8,12},{12,8},{9,1... | collective-permute-start | bytes 393224 | tf_op jit(solution)/shard_map/ppermute | solution.py:24
  94.6 92.5 %collective-permute-start.18 = (bf16[512,256]{0,1:T(8,128)(2,1)}, bf16[512,256]{0,1:T(8,128)(2,1)}, u32[]{:S(2)}, u32[]{:S(2)}) collective-permute-start(bf16[512,256]{0,1:T(8,128)(2,1)} %pad_maximum_fusion.26), channel_id=1, source_target_pairs={{0,16},{8,24},{16,0},{24,8},{1,17},{9,25},{17,1},{25,9},{2,18},{10... | collective-permute-start | bytes 786440 | tf_op jit(solution)/shard_map/ppermute | solution.py:20
  191.6 66.2 %collective-permute-start.24 = (f32[576,1024]{1,0:T(8,128)}, f32[576,1024]{1,0:T(8,128)}, u32[]{:S(2)}, u32[]{:S(2)}) collective-permute-start(f32[576,1024]{1,0:T(8,128)} %fusion.120), channel_id=1, source_target_pairs={{0,4},{4,0},{1,5},{5,1},{2,6},{6,2},{3,7},{7,3},{8,12},{12,8},{9,1... | collective-permute-start | bytes 7077896 | tf_op jit(solution)/shard_map/ppermute | solution.py:24
  238.4 28.7 %collective-permute-start.28 = (bf16[256,1024]{0,1:T(8,128)(2,1)S(1)}, bf16[256,1024]{0,1:T(8,128)(2,1)S(1)}, u32[]{:S(2)}, u32[]{:S(2)}) collective-permute-start(bf16[256,1024]{0,1:T(8,128)(2,1)S(1)} %pad_maximum_fusion.22), channel_id=1, source_target_pairs={{0,8},{8,0},{16,24},{24,16},{1,9},{9,1},{17,25},{25,17},{2,10},{10... | collective-permute-start | bytes 1572872 | tf_op jit(solution)/shard_map/ppermute | solution.py:20
  239.9 29.7 %collective-permute-start.32 = (bf16[256,1024]{0,1:T(8,128)(2,1)S(1)}, bf16[256,1024]{0,1:T(8,128)(2,1)S(1)}, u32[]{:S(2)}, u32[]{:S(2)}) collective-permute-start(bf16[256,1024]{0,1:T(8,128)(2,1)S(1)} %pad_maximum_fusion.23), channel_id=1, source_target_pairs={{0,8},{8,0},{16,24},{24,16},{1,9},{9,1},{17,25},{25,17},{2,10},{10... | collective-permute-start | bytes 1572872 | tf_op jit(solution)/shard_map/ppermute | solution.py:20
  245.1 39.5 %collective-permute-start.38 = (bf16[512,1024]{0,1:T(8,128)(2,1)}, bf16[512,1024]{0,1:T(8,128)(2,1)}, u32[]{:S(2)}, u32[]{:S(2)}) collective-permute-start(bf16[512,1024]{0,1:T(8,128)(2,1)} %pad_maximum_fusion.15), channel_id=1, source_target_pairs={{0,8},{8,0},{16,24},{24,16},{1,9},{9,1},{17,25},{25,17},{2,10},{10... | collective-permute-start | bytes 3145736 | tf_op jit(solution)/shard_map/ppermute | solution.py:20
  256.4 50.7 %collective-permute-start.43 = (bf16[512,1024]{0,1:T(8,128)(2,1)}, bf16[512,1024]{0,1:T(8,128)(2,1)}, u32[]{:S(2)}, u32[]{:S(2)}) collective-permute-start(bf16[512,1024]{0,1:T(8,128)(2,1)} %pad_maximum_fusion.16), channel_id=1, source_target_pairs={{0,8},{8,0},{16,24},{24,16},{1,9},{9,1},{17,25},{25,17},{2,10},{10... | collective-permute-start | bytes 3145736 | tf_op jit(solution)/shard_map/ppermute | solution.py:20
  262.9 45.5 %collective-permute-start.25 = (bf16[576,1024]{1,0:T(8,128)(2,1)}, bf16[576,1024]{1,0:T(8,128)(2,1)}, u32[]{:S(2)}, u32[]{:S(2)}) collective-permute-start(bf16[576,1024]{1,0:T(8,128)(2,1)} %fusion.47), channel_id=1, source_target_pairs={{0,4},{4,0},{1,5},{5,1},{2,6},{6,2},{3,7},{7,3},{8,12},{12,8},{9,1... | collective-permute-start | bytes 3538952 | tf_op jit(solution)/shard_map/ppermute | solution.py:24
  268.3 50.5 %collective-permute-start.29 = (bf16[512,1024]{0,1:T(8,128)(2,1)}, bf16[512,1024]{0,1:T(8,128)(2,1)}, u32[]{:S(2)}, u32[]{:S(2)}) collective-permute-start(bf16[512,1024]{0,1:T(8,128)(2,1)} %pad_maximum_fusion.13), channel_id=1, source_target_pairs={{0,16},{8,24},{16,0},{24,8},{1,17},{9,25},{17,1},{25,9},{2,18},{10... | collective-permute-start | bytes 3145736 | tf_op jit(solution)/shard_map/ppermute | solution.py:20
  270.7 55.3 %collective-permute-start.33 = (bf16[512,1024]{0,1:T(8,128)(2,1)}, bf16[512,1024]{0,1:T(8,128)(2,1)}, u32[]{:S(2)}, u32[]{:S(2)}) collective-permute-start(bf16[512,1024]{0,1:T(8,128)(2,1)} %pad_maximum_fusion.14), channel_id=1, source_target_pairs={{0,16},{8,24},{16,0},{24,8},{1,17},{9,25},{17,1},{25,9},{2,18},{10... | collective-permute-start | bytes 3145736 | tf_op jit(solution)/shard_map/ppermute | solution.py:20
  361.6 39.7 %collective-permute-start.49 = (bf16[576,1024]{1,0:T(8,128)(2,1)}, bf16[576,1024]{1,0:T(8,128)(2,1)}, u32[]{:S(2)}, u32[]{:S(2)}) collective-permute-start(bf16[576,1024]{1,0:T(8,128)(2,1)} %convert_element_type.286), channel_id=1, source_target_pairs={{0,4},{4,0},{1,5},{5,1},{2,6},{6,2},{3,7},{7,3},{8,12},{12,8},{9,1... | collective-permute-start | bytes 3538952 | tf_op jit(solution)/shard_map/ppermute | solution.py:24
  363.0 29.9 %collective-permute-start.45 = (bf16[288,1024]{1,0:T(8,128)(2,1)S(1)}, bf16[288,1024]{1,0:T(8,128)(2,1)S(1)}, u32[]{:S(2)}, u32[]{:S(2)}) collective-permute-start(bf16[288,1024]{1,0:T(8,128)(2,1)S(1)} %get-tuple-element.135), channel_id=1, source_target_pairs={{0,0},{1,1},{4,2},{5,3},{2,4},{3,5},{6,6},{7,7},{8,8},{9,9},{12,10... | collective-permute-start | bytes 1769480 | tf_op jit(solution)/shard_map/ppermute | solution.py:257
  397.4 127.7 %all-to-all-start.1 = ((bf16[8,72,1024]{2,1,0:T(8,128)(2,1)}), bf16[8,72,1024]{2,1,0:T(8,128)(2,1)S(1)}, u32[]{:S(2)}, u32[]{:S(2)}) async-start(bf16[8,72,1024]{2,1,0:T(8,128)(2,1)} %bitcast.127), calls=%async_computation.1 | async-start | bytes 2359296 | tf_op jit(solution)/shard_map/all_to_all | solution.py:263
  407.0 54.1 %collective-permute-start.91 = (bf16[512,1024]{0,1:T(8,128)(2,1)S(1)}, bf16[512,1024]{0,1:T(8,128)(2,1)S(1)}, u32[]{:S(2)}, u32[]{:S(2)}) collective-permute-start(bf16[512,1024]{0,1:T(8,128)(2,1)S(1)} %pad_maximum_fusion.18), channel_id=1, source_target_pairs={{0,8},{8,0},{16,24},{24,16},{1,9},{9,1},{17,25},{25,17},{2,10},{10... | collective-permute-start | bytes 3145736 | tf_op jit(solution)/shard_map/ppermute | solution.py:20
  414.0 48.6 %collective-permute-start.89 = (bf16[512,1024]{0,1:T(8,128)(2,1)S(1)}, bf16[512,1024]{0,1:T(8,128)(2,1)S(1)}, u32[]{:S(2)}, u32[]{:S(2)}) collective-permute-start(bf16[512,1024]{0,1:T(8,128)(2,1)S(1)} %concatenate.613), channel_id=1, source_target_pairs={{0,16},{8,24},{16,0},{24,8},{1,17},{9,25},{17,1},{25,9},{2,18},{10... | collective-permute-start | bytes 3145736 | tf_op jit(solution)/shard_map/ppermute | solution.py:20
  425.6 37.8 %collective-permute-start.82 = (bf16[512,1024]{0,1:T(8,128)(2,1)S(1)}, bf16[512,1024]{0,1:T(8,128)(2,1)S(1)}, u32[]{:S(2)}, u32[]{:S(2)}) collective-permute-start(bf16[512,1024]{0,1:T(8,128)(2,1)S(1)} %pad_maximum_fusion.17), channel_id=1, source_target_pairs={{0,8},{8,0},{16,24},{24,16},{1,9},{9,1},{17,25},{25,17},{2,10},{10... | collective-permute-start | bytes 3145736 | tf_op jit(solution)/shard_map/ppermute | solution.py:20
  440.4 23.8 %collective-permute-start.80 = (bf16[512,1024]{0,1:T(8,128)(2,1)S(1)}, bf16[512,1024]{0,1:T(8,128)(2,1)S(1)}, u32[]{:S(2)}, u32[]{:S(2)}) collective-permute-start(bf16[512,1024]{0,1:T(8,128)(2,1)S(1)} %concatenate.614), channel_id=1, source_target_pairs={{0,16},{8,24},{16,0},{24,8},{1,17},{9,25},{17,1},{25,9},{2,18},{10... | collective-permute-start | bytes 3145736 | tf_op jit(solution)/shard_map/ppermute | solution.py:20
  447.8 85.3 %collective-permute-start.50 = (f32[576,1024]{1,0:T(8,128)}, f32[576,1024]{1,0:T(8,128)}, u32[]{:S(2)}, u32[]{:S(2)}) collective-permute-start(f32[576,1024]{1,0:T(8,128)} %convolution_add_fusion.3), channel_id=1, source_target_pairs={{0,4},{4,0},{1,5},{5,1},{2,6},{6,2},{3,7},{7,3},{8,12},{12,8},{9,1... | collective-permute-start | bytes 7077896 | tf_op jit(solution)/shard_map/ppermute | solution.py:24
  464.4 29.2 %collective-permute-start.81 = (bf16[256,1024]{0,1:T(8,128)(2,1)S(1)}, bf16[256,1024]{0,1:T(8,128)(2,1)S(1)}, u32[]{:S(2)}, u32[]{:S(2)}) collective-permute-start(bf16[256,1024]{0,1:T(8,128)(2,1)S(1)} %fusion.75), channel_id=1, source_target_pairs={{0,8},{8,0},{16,24},{24,16},{1,9},{9,1},{17,25},{25,17},{2,10},{10... | collective-permute-start | bytes 1572872 | tf_op jit(solution)/shard_map/ppermute | solution.py:20
  494.0 26.9 %collective-permute-start.94 = (bf16[256,512]{0,1:T(8,128)(2,1)S(1)}, bf16[256,512]{0,1:T(8,128)(2,1)S(1)}, u32[]{:S(2)}, u32[]{:S(2)}) collective-permute-start(bf16[256,512]{0,1:T(8,128)(2,1)S(1)} %pad_maximum_fusion.31), channel_id=1, source_target_pairs={{0,1},{1,2},{2,3},{3,0},{4,5},{5,6},{6,7},{7,4},{8,9},{9,10},{10,1... | collective-permute-start | bytes 786440 | tf_op jit(solution)/shard_map/ppermute | solution.py:15
  715.6 32.5 %collective-permute-start.73 = (bf16[512,256]{1,0:T(8,128)(2,1)}, bf16[512,256]{1,0:T(8,128)(2,1)}, u32[]{:S(2)}, u32[]{:S(2)}) collective-permute-start(bf16[512,256]{1,0:T(8,128)(2,1)} %pad_maximum_fusion.28), channel_id=1, source_target_pairs={{0,8},{8,0},{16,24},{24,16},{1,9},{9,1},{17,25},{25,17},{2,10},{10... | collective-permute-start | bytes 786440 | tf_op jit(solution)/shard_map/ppermute | solution.py:20
  758.8 24.9 %collective-permute-start.57 = (bf16[512,768]{1,0:T(8,128)(2,1)S(1)}, bf16[512,768]{1,0:T(8,128)(2,1)S(1)}, u32[]{:S(2)}, u32[]{:S(2)}) collective-permute-start(bf16[512,768]{1,0:T(8,128)(2,1)S(1)} %pad_maximum_fusion.21), channel_id=1, source_target_pairs={{0,8},{8,0},{16,24},{24,16},{1,9},{9,1},{17,25},{25,17},{2,10},{10... | collective-permute-start | bytes 2359304 | tf_op jit(solution)/shard_map/ppermute | solution.py:20
  759.2 26.7 %collective-permute-start.55 = (bf16[512,768]{1,0:T(8,128)(2,1)S(1)}, bf16[512,768]{1,0:T(8,128)(2,1)S(1)}, u32[]{:S(2)}, u32[]{:S(2)}) collective-permute-start(bf16[512,768]{1,0:T(8,128)(2,1)S(1)} %concatenate.607), channel_id=1, source_target_pairs={{0,16},{8,24},{16,0},{24,8},{1,17},{9,25},{17,1},{25,9},{2,18},{10... | collective-permute-start | bytes 2359304 | tf_op jit(solution)/shard_map/ppermute | solution.py:20
  760.0 46.0 %collective-permute-start.52 = (f32[576,1024]{1,0:T(8,128)S(1)}, f32[576,1024]{1,0:T(8,128)S(1)}, u32[]{:S(2)}, u32[]{:S(2)}) collective-permute-start(f32[576,1024]{1,0:T(8,128)S(1)} %fusion.48), channel_id=1, source_target_pairs={{0,4},{4,0},{1,5},{5,1},{2,6},{6,2},{3,7},{7,3},{8,12},{12,8},{9,1... | collective-permute-start | bytes 7077896 | tf_op jit(solution)/shard_map/ppermute | solution.py:24
  809.1 24.7 %collective-permute-start.53 = (bf16[288,1024]{1,0:T(8,128)(2,1)}, bf16[288,1024]{1,0:T(8,128)(2,1)S(1)}, u32[]{:S(2)}, u32[]{:S(2)}) collective-permute-start(bf16[288,1024]{1,0:T(8,128)(2,1)} %get-tuple-element.119), channel_id=1, source_target_pairs={{0,0},{1,1},{4,2},{5,3},{2,4},{3,5},{6,6},{7,7},{8,8},{9,9},{12,10... | collective-permute-start | bytes 1769480 | tf_op jit(solution)/shard_map/ppermute | solution.py:257
  (255 other events, 3305.5 us)

commit v2 on v1

v2 whole, which is shorter than its diff:
```python
import functools

import jax
import jax.numpy as jnp
from jax import lax
from jax.experimental import pallas as pl
from jax.experimental.pallas import tpu as pltpu
from jax.sharding import Mesh, PartitionSpec as P

DH = 64
MB = 2
F32 = jnp.float32
BF16 = jnp.bfloat16
ALL = ("chip", "core", "tensor")
MESH = pl.DeviceIdType.MESH
ANY = pl.BlockSpec(memory_space=pl.ANY)
IN_VMEM = pl.BlockSpec(memory_space=pltpu.VMEM)


def swap(x):
    return lax.ppermute(x, "core", [(0, 1), (1, 0)])


def flip(x, bit):
    n = lax.axis_size("chip")
    return lax.ppermute(x, "chip", [(i, i ^ bit) for i in range(n)])


def chip_bits():
    n = lax.axis_size("chip")
    return [1 << i for i in range(n.bit_length() - 1)]


class Place:
    def __init__(self, chips, ways):
        self.chip = lax.axis_index("chip")
        self.core = lax.axis_index("core")
        self.line = lax.axis_index("tensor")
        self.ways = ways
        self.count = chips.bit_length() - 1
        self.bits = [lax.rem(self.chip // (1 << i), 2) for i in range(self.count)]

    def other_core(self):
        return {"core": 1 - self.core}

    def along(self, step):
        return {"tensor": lax.rem(self.line + step + self.ways, self.ways)}

    def across(self, i):
        return {"chip": self.chip + (1 - 2 * self.bits[i]) * (1 << i)}

    def unit(self, step):
        return lax.rem(self.line + step + self.ways, self.ways)

    def greet(self):
        barrier = pltpu.get_barrier_semaphore()
        partners = [self.other_core(), self.along(1), self.along(-1)]
        partners += [self.across(i) for i in range(self.count)]
        for partner in partners:
            pl.semaphore_signal(barrier, inc=1, device_id=partner, device_id_type=MESH)
        pl.semaphore_wait(barrier, len(partners))

    def blocks(self, free, flipped=None):
        index = []
        for i in reversed(range(self.count)):
            if i in free:
                index.append(slice(None))
            elif i == flipped:
                index.append(1 - self.bits[i])
            else:
                index.append(self.bits[i])
        return tuple(index)


UNITS = (0, -1, 1, 2)


def unit_bits(u, count):
    order = list(range(count))
    return order if u in (0, 3) else order[::-1]


def remote(src, dst, send, recv, where):
    return pltpu.make_async_remote_copy(
        src_ref=src,
        dst_ref=dst,
        send_sem=send,
        recv_sem=recv,
        device_id=where,
        device_id_type=MESH,
    )


def columns(index, width):
    return pl.ds(pl.multiple_of(index * width, width), width)


def row_span(index, depth):
    return pl.ds(pl.multiple_of(index * depth, depth), depth)


class Gather:
    def __init__(self, place, shard, whole, piece, sends, recvs, own_sem):
        self.place, self.shard, self.whole, self.piece = place, shard, whole, piece
        self.sends, self.recvs, self.own_sem = sends, recvs, own_sem
        self.width = piece.shape[1]
        self.depth = shard.shape[0]
        self.copies = []

    def slot(self, u):
        return columns(self.place.unit(UNITS[u]), self.width)

    def launch(self, number, src, dst, where):
        copy = remote(src, dst, self.sends.at[number], self.recvs.at[number], where)
        copy.start()
        self.copies.append(copy)
        return copy

    def pair(self):
        p = self.place
        mine = row_span(p.core, self.depth)
        self.keep = pltpu.make_async_copy(
            self.shard.at[:, columns(p.core, self.width)], self.piece.at[mine], self.own_sem.at[0]
        )
        self.keep.start()
        self.pair_copy = self.launch(
            0, self.shard.at[:, columns(1 - p.core, self.width)], self.piece.at[mine], p.other_core()
        )

    def open(self):
        p = self.place
        self.keep.wait()
        self.pair_copy.wait_recv()
        here = self.whole.at[p.blocks(()) + (slice(None), self.slot(0))]
        self.settle = pltpu.make_async_copy(self.piece, here, self.own_sem.at[1])
        self.settle.start()
        self.below = self.launch(1, self.piece, here, p.along(1))
        self.above = self.launch(2, self.piece, here, p.along(-1))
        self.stages = [[None] * p.count for _ in range(4)]
        self.across(0, 0, self.piece)

    def across(self, u, stage, src=None):
        p = self.place
        if p.count == 0:
            return
        order = unit_bits(u, p.count)
        where = self.whole.at[p.blocks(order[:stage]) + (slice(None), self.slot(u))]
        self.stages[u][stage] = self.launch(
            5 + u * p.count + stage,
            where if src is None else src,
            where,
            p.across(order[stage]),
        )

    def half(self, u, part):
        rows = pl.ds(part * self.depth, self.depth)
        return self.whole.at[self.place.blocks(()) + (rows, self.slot(u))]

    def line_below(self):
        self.below.wait_recv()
        self.far_low = self.launch(3, self.half(1, 0), self.half(1, 0), self.place.along(1))
        self.across(1, 0)

    def line_above(self):
        self.above.wait_recv()
        self.far_high = self.launch(4, self.half(2, 1), self.half(2, 1), self.place.along(-1))
        self.across(2, 0)

    def line_far(self):
        self.far_low.wait_recv()
        self.far_high.wait_recv()
        self.across(3, 0)

    def forward(self, u, stage):
        self.stages[u][stage - 1].wait_recv()
        if u == 0 and stage == 1:
            self.settle.wait()
        self.across(u, stage)

    def finish(self):
        if self.place.count < 2:
            self.settle.wait()
        for u in range(4):
            if self.place.count:
                self.stages[u][-1].wait_recv()
        for copy in self.copies:
            copy.wait_send()


def gather_steps(works, count):
    steps = []
    for w in works:
        steps.append(w.pair)
    for w in works:
        steps.append(w.open)
    for w in works:
        steps.append(w.line_below)
        steps.append(w.line_above)
    for stage in range(1, count):
        for u in (0, 1, 2):
            for w in works:
                if stage == 1 and u == 1:
                    steps.append(w.line_far)
                steps.append(functools.partial(w.forward, u, stage))
    if count < 2:
        for w in works:
            steps.append(w.line_far)
    for stage in range(1, count):
        for w in works:
            steps.append(functools.partial(w.forward, 3, stage))
    for w in works:
        steps.append(w.finish)
    return steps


def gather_kernel(chips, ways, number, *refs):
    place = Place(chips, ways)
    shards, refs = refs[:number], refs[number:]
    wholes, refs = refs[:number], refs[number:]
    pieces, refs = refs[:number], refs[number:]
    sends, recvs, own = refs
    place.greet()
    works = [
        Gather(place, shards[i], wholes[i], pieces[i], sends.at[i], recvs.at[i], own.at[i])
        for i in range(number)
    ]
    for step in gather_steps(works, place.count):
        step()


def gather_weights(shards, chips, ways, collective_id):
    bits = chips.bit_length() - 1
    number = len(shards)
    sems = 5 + 4 * bits
    wholes = pl.pallas_call(
        functools.partial(gather_kernel, chips, ways, number),
        in_specs=[ANY] * number,
        out_specs=[ANY] * number,
        out_shape=[
            jax.ShapeDtypeStruct(
                (2,) * bits + (2 * s.shape[0], ways * s.shape[1] // 2), s.dtype
            )
            for s in shards
        ],
        scratch_shapes=[
            pltpu.VMEM((2 * s.shape[0], s.shape[1] // 2), s.dtype) for s in shards
        ]
        + [
            pltpu.SemaphoreType.DMA((number, sems)),
            pltpu.SemaphoreType.DMA((number, sems)),
            pltpu.SemaphoreType.DMA((number, 2)),
        ],
        name="gather_weights",
        compiler_params=pltpu.CompilerParams(
            collective_id=collective_id, has_side_effects=True, vmem_limit_bytes=32 << 20
        ),
    )(*shards)
    return [w.reshape(-1, w.shape[-1]) for w in wholes]


class Scatter:
    def __init__(self, place, whole, shard, mine, slots, temps, keeps, line, last, sems):
        self.place, self.whole, self.shard = place, whole, shard
        self.mine, self.slots, self.temps, self.keeps = mine, slots, temps, keeps
        self.line_in, self.line_out, self.final = line
        self.far_in = last
        self.sends, self.recvs, self.own = sems
        self.width = shard.shape[1] // 2
        self.depth = shard.shape[0]
        self.copies = []
        self.stages = [[None] * place.count for _ in range(4)]

    def launch(self, number, src, dst, where):
        copy = remote(src, dst, self.sends.at[number], self.recvs.at[number], where)
        copy.start()
        self.copies.append(copy)
        return copy

    def slot(self, u):
        return columns(self.place.unit(UNITS[u]), self.width)

    def open(self, u):
        p = self.place
        order = unit_bits(u, p.count)
        first = order[0]
        lanes = (slice(None), self.slot(u))
        self.stages[u][0] = self.launch(
            u * p.count,
            self.whole.at[p.blocks(order[1:], first) + lanes],
            self.slots[0].at[u],
            p.across(first),
        )
        copy = pltpu.make_async_copy(
            self.whole.at[p.blocks(order[1:]) + lanes], self.mine.at[u], self.own.at[u]
        )
        copy.start()
        self.stages[u].append(copy)

    def chip_index(self, u, stage, other):
        p = self.place
        order = unit_bits(u, p.count)
        left = order[stage:]
        index = []
        for i in sorted(left, reverse=True):
            if i == left[0]:
                index.append(1 - p.bits[i] if other else p.bits[i])
            else:
                index.append(slice(None))
        return tuple(index)

    def forward(self, u, stage):
        p = self.place
        order = unit_bits(u, p.count)
        self.stages[u][stage - 1].wait_recv()
        if stage == 1:
            self.stages[u][-1].wait()
        source = self.mine if stage == 1 else self.keeps[stage - 1]
        there = (u,) + self.chip_index(u, stage, True)
        here = (u,) + self.chip_index(u, stage, False)
        arrived = self.slots[stage - 1]
        self.temps[stage - 1][u] = (
            source[there].astype(F32) + arrived[there].astype(F32)
        ).astype(BF16)
        self.stages[u][stage] = self.launch(
            u * p.count + stage,
            self.temps[stage - 1].at[u],
            self.slots[stage].at[u],
            p.across(order[stage]),
        )
        self.keeps[stage][u] = source[here].astype(F32) + arrived[here].astype(F32)

    def total(self, u):
        p = self.place
        last = p.count - 1
        self.stages[u][last].wait_recv()
        if last == 0:
            self.stages[u][-1].wait()
            return self.mine[u].astype(F32) + self.slots[0][u].astype(F32)
        return self.keeps[last][u] + self.slots[last][u].astype(F32)

    def line_far(self):
        p = self.place
        base = 4 * p.count
        self.far_in[0] = self.total(3).astype(BF16)
        low, high = pl.ds(0, self.depth), pl.ds(self.depth, self.depth)
        self.low = self.launch(
            base, self.far_in.at[0, low], self.far_in.at[1, low], p.along(1)
        )
        self.high = self.launch(
            base + 1, self.far_in.at[0, high], self.far_in.at[1, high], p.along(-1)
        )

    def line_above(self):
        p = self.place
        base = 4 * p.count
        depth = self.depth
        total = self.total(2)
        self.low.wait_recv()
        self.line_out[0, :depth] = (total[:depth] + self.far_in[1, :depth].astype(F32)).astype(
            BF16
        )
        self.line_out[0, depth:] = total[depth:].astype(BF16)
        self.from_below = self.launch(
            base + 2, self.line_out.at[0], self.line_in.at[0], p.along(1)
        )

    def line_below(self):
        p = self.place
        base = 4 * p.count
        depth = self.depth
        total = self.total(1)
        self.high.wait_recv()
        self.line_out[1, depth:] = (total[depth:] + self.far_in[1, depth:].astype(F32)).astype(
            BF16
        )
        self.line_out[1, :depth] = total[:depth].astype(BF16)
        self.from_above = self.launch(
            base + 3, self.line_out.at[1], self.line_in.at[1], p.along(-1)
        )

    def close(self):
        p = self.place
        total = self.total(0)
        self.from_below.wait_recv()
        self.from_above.wait_recv()
        self.final[...] = total + self.line_in[0].astype(F32) + self.line_in[1].astype(F32)
        lanes = columns(p.core, self.width)
        self.pair = self.launch(
            4 * p.count + 4,
            self.final.at[row_span(1 - p.core, self.depth)],
            self.shard.at[:, lanes],
            p.other_core(),
        )
        self.keep = pltpu.make_async_copy(
            self.final.at[row_span(p.core, self.depth)], self.shard.at[:, lanes], self.own.at[4]
        )
        self.keep.start()

    def finish(self):
        self.keep.wait()
        self.pair.wait_recv()
        for copy in self.copies:
            copy.wait_send()


def scatter_steps(works, count):
    steps = []
    for u in (3, 2, 1, 0):
        for w in works:
            steps.append(functools.partial(w.open, u))
    for stage in range(1, count):
        for u in (3, 2, 1, 0):
            for w in works:
                steps.append(functools.partial(w.forward, u, stage))
    for name in ("line_far", "line_above", "line_below", "close", "finish"):
        for w in works:
            steps.append(getattr(w, name))
    return steps


def scatter_scratch(depth, width, bits):
    shapes = []
    for stage in range(bits):
        left = (2,) * (bits - 1 - stage)
        shapes.append(pltpu.VMEM((4,) + left + (2 * depth, width), BF16))
    shapes.append(pltpu.VMEM((4,) + (2,) * (bits - 1) + (2 * depth, width), BF16))
    for stage in range(1, bits):
        left = (2,) * (bits - 1 - stage)
        shapes.append(pltpu.VMEM((4,) + left + (2 * depth, width), BF16))
        shapes.append(pltpu.VMEM((4,) + left + (2 * depth, width), F32))
    shapes.append(pltpu.VMEM((2, 2 * depth, width), BF16))
    shapes.append(pltpu.VMEM((2, 2 * depth, width), BF16))
    shapes.append(pltpu.VMEM((2, 2 * depth, width), BF16))
    shapes.append(pltpu.VMEM((2 * depth, width), F32))
    return shapes


def scatter_work(place, whole, shard, scratch, sems):
    count = place.count
    scratch = list(scratch)
    slots = [scratch.pop(0) for _ in range(count)]
    mine = scratch.pop(0)
    temps, keeps = [], [None]
    for _ in range(1, count):
        temps.append(scratch.pop(0))
        keeps.append(scratch.pop(0))
    line_in, line_out, far_in, final = scratch
    return Scatter(
        place, whole, shard, mine, slots, temps, keeps, (line_in, line_out, final), far_in, sems
    )


def scatter_kernel(chips, ways, number, *refs):
    place = Place(chips, ways)
    wholes, refs = refs[:number], refs[number:]
    shards, refs = refs[:number], refs[number:]
    sends, recvs, own = refs[-3:]
    each = (len(refs) - 3) // number
    place.greet()
    works = [
        scatter_work(
            place,
            wholes[i],
            shards[i],
            refs[i * each : (i + 1) * each],
            (sends.at[i], recvs.at[i], own.at[i]),
        )
        for i in range(number)
    ]
    for step in scatter_steps(works, place.count):
        step()


def scatter_grads(grads, chips, ways, collective_id):
    bits = chips.bit_length() - 1
    number = len(grads)
    shapes = [(g.shape[0] // (2 * chips), g.shape[1] // ways) for g in grads]
    scratch = []
    for depth, width in shapes:
        scratch += scatter_scratch(depth, width, bits)
    sems = 4 * bits + 5
    return pl.pallas_call(
        functools.partial(scatter_kernel, chips, ways, number),
        in_specs=[ANY] * number,
        out_specs=[ANY] * number,
        out_shape=[jax.ShapeDtypeStruct((depth, 2 * width), F32) for depth, width in shapes],
        scratch_shapes=scratch
        + [
            pltpu.SemaphoreType.DMA((number, sems)),
            pltpu.SemaphoreType.DMA((number, sems)),
            pltpu.SemaphoreType.DMA((number, 5)),
        ],
        name="scatter_grads",
        compiler_params=pltpu.CompilerParams(
            collective_id=collective_id, has_side_effects=True, vmem_limit_bytes=48 << 20
        ),
    )(
        *[
            g.reshape((2,) * bits + (2 * depth, g.shape[1]))
            for g, (depth, _) in zip(grads, shapes)
        ]
    )


def head_lanes(shape, h):
    lanes = lax.broadcasted_iota(jnp.int32, shape, 1)
    return (lanes // DH) == h


def attention_forward_kernel(qkv_ref, col_ref, row_ref, o_ref, lse_ref, vt_ref):
    k = qkv_ref[:, 128:256]
    vt_ref[...] = qkv_ref[:, 256:384].astype(F32).T.astype(BF16)
    q = qkv_ref[:, 0:128] * jnp.asarray(DH**-0.5, BF16)
    same = col_ref[...] == row_ref[...]
    outs = []
    for h in range(2):
        q_h = jnp.where(head_lanes(q.shape, h), q, jnp.zeros_like(q))
        s = jnp.where(same, nt(k, q_h), -1e30)
        top = jnp.max(s, axis=0, keepdims=True)
        p = jnp.exp(s - top)
        total = jnp.sum(p, axis=0, keepdims=True)
        low = (p * (1.0 / total)).astype(BF16)
        outs.append(nn(vt_ref[h * DH : (h + 1) * DH], low))
        lse_ref[0, h : h + 1, :] = top + jnp.log(total)
    o_ref[...] = jnp.concatenate(outs, 0).T.astype(BF16)


def attention_forward(qkv, seq):
    count = qkv.shape[0]
    pairs = qkv.shape[1] // 384
    return pl.pallas_call(
        attention_forward_kernel,
        grid=(pairs,),
        in_specs=[
            pl.BlockSpec((count, 384), lambda p: (0, p)),
            pl.BlockSpec((count, 1), lambda p: (0, 0)),
            pl.BlockSpec((1, count), lambda p: (0, 0)),
        ],
        out_specs=[
            pl.BlockSpec((count, 128), lambda p: (0, p)),
            pl.BlockSpec((1, 2, count), lambda p: (p, 0, 0)),
        ],
        out_shape=[
            jax.ShapeDtypeStruct((count, pairs * 128), BF16),
            jax.ShapeDtypeStruct((pairs, 2, count), F32),
        ],
        scratch_shapes=[pltpu.VMEM((128, count), BF16)],
        name="attention_forward",
        cost_estimate=pl.CostEstimate(
            flops=pairs * 2 * 4 * count * count * 256,
            bytes_accessed=qkv.size * 2 + count * pairs * 256,
            transcendentals=pairs * 2 * count * count,
        ),
        compiler_params=pltpu.CompilerParams(
            dimension_semantics=("arbitrary",), vmem_limit_bytes=56 << 20
        ),
    )(qkv, seq[:, None], seq[None, :])


def attention_backward_kernel(
    qkv_ref, do_ref, lse_ref, col_ref, row_ref, dqkv_ref, qb_ref, vb_ref, kt_ref
):
    k = qkv_ref[:, 128:256]
    v = qkv_ref[:, 256:384]
    kt_ref[...] = k.astype(F32).T.astype(BF16)
    q = qkv_ref[:, 0:128] * jnp.asarray(DH**-0.5, BF16)
    do = do_ref[...]
    same = col_ref[...] == row_ref[...]
    dq_t, dk, dv = [], None, None
    for h in range(2):
        keep = head_lanes(q.shape, h)
        q_h = jnp.where(keep, q, jnp.zeros_like(q))
        do_h = jnp.where(keep, do, jnp.zeros_like(do))
        s_t = jnp.where(same, nt(k, q_h), -1e30)
        p_t = jnp.exp(s_t - lse_ref[0, h : h + 1, :])
        dp_t = nt(v, do_h)
        delta = jnp.sum(dp_t * p_t, axis=0, keepdims=True)
        dv_h = nn(p_t.astype(BF16), do_h)
        ds_t = (p_t * (dp_t - delta)).astype(BF16)
        dk_h = nn(ds_t, q_h)
        dq_t.append(nn(kt_ref[h * DH : (h + 1) * DH], ds_t))
        dk = dk_h if dk is None else dk + dk_h
        dv = dv_h if dv is None else dv + dv_h
    dq = jnp.concatenate(dq_t, 0).T * (DH**-0.5)
    dqkv_ref[:, 0:128] = dq.astype(BF16)
    dqkv_ref[:, 128:256] = dk.astype(BF16)
    dqkv_ref[:, 256:384] = dv.astype(BF16)
    qb_ref[...] = jnp.broadcast_to(jnp.sum(dq, axis=0, keepdims=True)[None], qb_ref.shape)
    vb_ref[...] = jnp.broadcast_to(jnp.sum(dv, axis=0, keepdims=True)[None], vb_ref.shape)


def attention_backward(qkv, d_out, lse, seq):
    count = qkv.shape[0]
    pairs = qkv.shape[1] // 384
    dqkv, qb, vb = pl.pallas_call(
        attention_backward_kernel,
        grid=(pairs,),
        in_specs=[
            pl.BlockSpec((count, 384), lambda p: (0, p)),
            pl.BlockSpec((count, 128), lambda p: (0, p)),
            pl.BlockSpec((1, 2, count), lambda p: (p, 0, 0)),
            pl.BlockSpec((count, 1), lambda p: (0, 0)),
            pl.BlockSpec((1, count), lambda p: (0, 0)),
        ],
        out_specs=[
            pl.BlockSpec((count, 384), lambda p: (0, p)),
            pl.BlockSpec((1, 8, 128), lambda p: (p, 0, 0)),
            pl.BlockSpec((1, 8, 128), lambda p: (p, 0, 0)),
        ],
        out_shape=[
            jax.ShapeDtypeStruct((count, pairs * 384), BF16),
            jax.ShapeDtypeStruct((pairs, 8, 128), F32),
            jax.ShapeDtypeStruct((pairs, 8, 128), F32),
        ],
        scratch_shapes=[pltpu.VMEM((128, count), BF16)],
        name="attention_backward",
        cost_estimate=pl.CostEstimate(
            flops=pairs * 2 * 10 * count * count * 256,
            bytes_accessed=qkv.size * 4 + count * pairs * 256,
            transcendentals=pairs * 2 * count * count,
        ),
        compiler_params=pltpu.CompilerParams(
            dimension_semantics=("arbitrary",), vmem_limit_bytes=60 << 20
        ),
    )(qkv, d_out, lse, seq[:, None], seq[None, :])
    return dqkv, qb[:, 0], vb[:, 0]


def exchange_sum(make_part):
    there = swap(make_part(True))
    return make_part(False) + there


def inverse_of(slots):
    count = slots.shape[0]
    marks = jnp.arange(count, dtype=jnp.int32)
    hit = slots[None, :] == marks[:, None]
    return jnp.sum(jnp.where(hit, marks[None, :], 0), axis=1)


def normalize(values):
    center = values - jnp.mean(values, axis=-1, keepdims=True)
    spread = jnp.mean(center * center, axis=-1, keepdims=True)
    inverse = lax.rsqrt(spread + 1e-05)
    return center * inverse, inverse


def norm_back(grad, normed, inverse, gain):
    scaled = grad * gain
    mean_one = jnp.mean(scaled, axis=-1, keepdims=True)
    mean_two = jnp.mean(scaled * normed, axis=-1, keepdims=True)
    return inverse * (scaled - mean_one - normed * mean_two)


def nn(x, y):
    return jnp.dot(x, y, preferred_element_type=F32)


def nt(x, y):
    return lax.dot_general(x, y, (((1,), (1,)), ((), ())), preferred_element_type=F32)


def tn(x, y):
    return lax.dot_general(x, y, (((0,), (0,)), ((), ())), preferred_element_type=F32)


def gelu_both(z):
    gate = 0.5 * (1.0 + lax.erf(z * 0.7071067811865476))
    slope = gate + z * jnp.exp(-0.5 * z * z) * 0.3989422804014327
    return z * gate, slope


def on_device(
    tokens,
    cotangent,
    deal,
    source,
    lengths,
    qkv_weight,
    query_bias,
    value_bias,
    out_weight,
    out_bias,
    first_gain,
    first_shift,
    up_weight,
    up_bias,
    down_weight,
    down_bias,
    second_gain,
    second_shift,
):
    core = lax.axis_index("core")
    line = lax.axis_index("tensor")
    ways = lax.axis_size("tensor")
    chips = lax.axis_size("chip")
    data_ways = 2 * chips
    rows, width = tokens.shape
    per_peer = rows // data_ways
    group_rows = ways * rows
    quarter = rows // MB
    dp = ("chip", "core")

    targets = deal // group_rows
    one_hot = (targets[:, None] == jnp.arange(data_ways, dtype=jnp.int32)[None, :]).astype(
        jnp.int32
    )
    send_slot = targets * per_peer + jnp.sum(one_hot * jnp.cumsum(one_hot, axis=0), axis=1) - 1
    senders = source // group_rows
    earlier = (senders[:, None] == senders[None, :]) & (source[None, :] < source[:, None])
    recv_slot = senders * per_peer + jnp.sum(earlier.astype(jnp.int32), axis=1)
    odd = line % 2
    first_rows = lax.dynamic_slice_in_dim(recv_slot, odd * quarter, quarter)
    second_rows = lax.dynamic_slice_in_dim(recv_slot, (1 - odd) * quarter, quarter)
    recv_order = jnp.concatenate([first_rows, second_rows])
    send_order = inverse_of(send_slot)
    back_order = inverse_of(recv_order)

    def moves(which):
        pairs = []
        for k in range(2):
            for t in range(ways):
                m = t % 2 if which == 0 else 1 - t % 2
                pairs.append((k * ways + t, (t // 2) * ways + 2 * k + m))
        return pairs

    def to_owner(x):
        outgoing = x[send_order]
        arrived = lax.all_to_all(outgoing, dp, split_axis=0, concat_axis=0, tiled=True)
        work = arrived[recv_order]
        return jnp.concatenate(
            [
                lax.ppermute(work[:quarter], ("core", "tensor"), moves(0)),
                lax.ppermute(work[quarter:], ("core", "tensor"), moves(1)),
            ],
            0,
        )

    def from_owner(x):
        back = [[(b, a) for a, b in moves(which)] for which in range(2)]
        work = jnp.concatenate(
            [
                lax.ppermute(x[:quarter], ("core", "tensor"), back[0]),
                lax.ppermute(x[quarter:], ("core", "tensor"), back[1]),
            ],
            0,
        )
        outgoing = work[back_order]
        arrived = lax.all_to_all(outgoing, dp, split_axis=0, concat_axis=0, tiled=True)
        return arrived[send_slot]

    depth = qkv_weight.shape[1]
    unit = qkv_weight.shape[2] // 2
    qkv_shard = (
        qkv_weight.reshape(3, depth, 2, unit).transpose(1, 2, 0, 3).reshape(depth, 6 * unit)
    )
    (qkv_w,) = gather_weights([qkv_shard], chips, ways, 0)
    rows_x = to_owner(tokens)
    out_w, up_w, down_w = gather_weights([out_weight.T, up_weight, down_weight.T], chips, ways, 1)

    which_group = line // 2
    lengths_here = jnp.where(core == which_group, lengths[0], swap(lengths[0]))
    seq_ends = jnp.cumsum(lax.dynamic_index_in_dim(lengths_here, odd, 0, keepdims=False))
    steps = jnp.arange(quarter, dtype=jnp.int32)
    positions = jnp.concatenate(
        [(2 * c + b) * quarter + steps for c in (core, 1 - core) for b in (odd, 1 - odd)]
    )
    seq_ids = jnp.sum((positions[:, None] >= seq_ends[None, :]).astype(jnp.int32), axis=1)

    def local_half(vector):
        parts = vector.astype(F32).reshape(ways, 2, -1)
        return lax.dynamic_index_in_dim(parts, core, 1, keepdims=False)

    def placed_half(parts):
        here = jnp.arange(2)[None, :, None] == core
        return jnp.where(here, parts[:, None, :], 0.0).reshape(-1)

    query_half, value_half = local_half(query_bias), local_half(value_bias)
    qkv_bias = jnp.stack([query_half, jnp.zeros_like(query_half), value_half], 1).reshape(-1)
    up_local = local_half(up_bias).reshape(-1)
    out_bias_f, first_gain_f, first_shift_f, down_bias_f, second_gain_f, second_shift_f = (
        v.astype(F32)
        for v in (out_bias, first_gain, first_shift, down_bias, second_gain, second_shift)
    )

    pair_x = jnp.concatenate([rows_x, swap(rows_x)], 0)
    projected = (nn(pair_x, qkv_w) + qkv_bias).astype(BF16)
    mixed, lse = attention_forward(projected, seq_ids)
    first_sum = (
        rows_x.astype(F32)
        + exchange_sum(lambda other: nt(mixed[rows:] if other else mixed[:rows], out_w))
        + out_bias_f
    )
    first_normed, first_inverse = normalize(first_sum)
    first_out = first_normed * first_gain_f + first_shift_f
    first_low = first_out.astype(BF16)
    pair_y = jnp.concatenate([first_low, swap(first_low)], 0)
    hidden, slope = gelu_both(nn(pair_y, up_w) + up_local)
    hidden = hidden.astype(BF16)
    second_sum = (
        first_out
        + exchange_sum(lambda other: nt(hidden[rows:] if other else hidden[:rows], down_w))
        + down_bias_f
    )
    second_normed, second_inverse = normalize(second_sum)
    result = (second_normed * second_gain_f + second_shift_f).astype(BF16)

    rows_g = to_owner(cotangent).astype(F32)
    second_back = norm_back(rows_g, second_normed, second_inverse, second_gain_f)
    second_gain_grad = jnp.sum(rows_g * second_normed, axis=0)
    second_shift_grad = jnp.sum(rows_g, axis=0)
    down_bias_grad = jnp.sum(second_back, axis=0)
    second_low = second_back.astype(BF16)
    pair_m = jnp.concatenate([second_low, swap(second_low)], 0)
    down_grad = tn(pair_m, hidden).astype(BF16)
    pre = nn(pair_m, down_w) * slope
    up_bias_local = jnp.sum(pre, axis=0)
    pre = pre.astype(BF16)
    up_grad = tn(pair_y, pre).astype(BF16)
    first_grad = second_back + exchange_sum(
        lambda other: nt(pre[rows:] if other else pre[:rows], up_w)
    )
    down_shard, up_shard = scatter_grads([down_grad, up_grad], chips, ways, 2)
    first_back = norm_back(first_grad, first_normed, first_inverse, first_gain_f)
    first_gain_grad = jnp.sum(first_grad * first_normed, axis=0)
    first_shift_grad = jnp.sum(first_grad, axis=0)
    out_bias_grad = jnp.sum(first_back, axis=0)
    first_back_low = first_back.astype(BF16)
    pair_o = jnp.concatenate([first_back_low, swap(first_back_low)], 0)
    out_grad = tn(pair_o, mixed).astype(BF16)
    mixed_back = nn(pair_o, out_w).astype(BF16)
    proj_back, query_bias_local, value_bias_local = attention_backward(
        projected, mixed_back, lse, seq_ids
    )
    qkv_grad = tn(pair_x, proj_back).astype(BF16)
    out_shard, qkv_shard = scatter_grads([out_grad, qkv_grad], chips, ways, 3)
    input_back = first_back + exchange_sum(
        lambda other: nt(proj_back[rows:] if other else proj_back[:rows], qkv_w)
    )

    layer_out = from_owner(result)
    tokens_grad = from_owner(input_back.astype(BF16)).astype(F32)

    feature = [
        out_bias_grad,
        first_gain_grad,
        first_shift_grad,
        down_bias_grad,
        second_gain_grad,
        second_shift_grad,
    ]
    placed = [
        placed_half(query_bias_local),
        placed_half(value_bias_local),
        placed_half(up_bias_local.reshape(ways, -1)),
    ]
    packed = jnp.concatenate(feature + placed).reshape(-1, 128)
    packed = packed + swap(packed)
    for bit in chip_bits():
        packed = packed + flip(packed, bit)
    step = 1
    while step < ways:
        packed = packed + lax.ppermute(packed, "tensor", [(i, i ^ step) for i in range(ways)])
        step *= 2
    packed = packed.reshape(-1)
    sizes = [v.shape[0] for v in feature + placed]
    ends = [sum(sizes[: i + 1]) for i in range(len(sizes))]
    (
        out_bias_grad,
        first_gain_grad,
        first_shift_grad,
        down_bias_grad,
        second_gain_grad,
        second_shift_grad,
        query_bias_grad,
        value_bias_grad,
        up_bias_grad,
    ) = (packed[end - size : end] for end, size in zip(ends, sizes))
    return (
        layer_out,
        tokens_grad,
        qkv_shard.reshape(depth, 2, 3, unit).transpose(2, 0, 1, 3).reshape(3, depth, 2 * unit),
        query_bias_grad,
        value_bias_grad,
        out_shard.T,
        out_bias_grad,
        first_gain_grad,
        first_shift_grad,
        up_shard,
        up_bias_grad,
        down_shard.T,
        down_bias_grad,
        second_gain_grad,
        second_shift_grad,
    )


def solution(mesh):
    data_ways, split_ways = mesh.shape["dp"], mesh.shape["tensor"]
    fine = Mesh(mesh.devices.reshape(data_ways // 2, 2, split_ways), ALL)
    dp = ("chip", "core")
    in_specs = (
        P(ALL, None),
        P(ALL, None),
        P(ALL),
        P(ALL),
        P(dp, None, None),
        P(None, dp, "tensor"),
        P(),
        P(),
        P("tensor", dp),
        P(),
        P(),
        P(),
        P(dp, "tensor"),
        P(),
        P("tensor", dp),
        P(),
        P(),
        P(),
    )
    out_specs = (
        P(ALL, None),
        P(ALL, None),
        P(None, dp, "tensor"),
        P(),
        P(),
        P("tensor", dp),
        P(),
        P(),
        P(),
        P(dp, "tensor"),
        P(),
        P("tensor", dp),
        P(),
        P(),
        P(),
    )
    return jax.shard_map(
        on_device, mesh=fine, in_specs=in_specs, out_specs=out_specs, check_vma=False
    )
```

time: 877 us -> 650 us (0.74); the launches traced: 861 us -> 646 us
  Pallas kernels: 0 us -> 343 us
  matrix products: 300 us -> 90.7 us
  starting transfers between devices: 182 us -> 65.2 us
  waiting for transfers between devices: 187 us -> 75.1 us
  other arithmetic: 98.8 us -> 17.9 us
  local copies, waits for them, and re-layouts: 89.5 us -> 52.3 us
    pallas_call x0 -> x6, Pallas kernels: none -> 343 us  [the longest x2 146 us: gather_weights(): pl.pallas_call(functools.partial(gather_kernel, chips, ways, number), in_...]
    dot_general x6 -> x0, matrix products: 199 us -> none  [the longest x1 67.2 us: on_device(): jnp.einsum('hqk,qhd->khd', score_back, queries, preferred_element_type=F32)]
    ppermute x34 -> x2, waiting for transfers between devices: 79.5 us -> 5.85 us  [flip(): return lax.ppermute(x, 'chip', [(i, i ^ bit) for i in range(n)])]
    ppermute x34 -> x2, starting transfers between devices: 73 us -> 3.15 us  [on_device(): lax.ppermute(packed, 'tensor', [(i, i ^ step) for i in range(ways)])]
    ppermute x2, waiting for transfers between devices: 38 us -> 0.01 us  [from_owner(): lax.ppermute(x[:quarter], ('core', 'tensor'), back[0])]
    concatenate x35 -> x2, other arithmetic: 39.8 us -> 2.42 us  [from_owner(): jnp.concatenate([lax.ppermute(x[:quarter], ('core', 'tensor'), back[0]),...]
    ppermute x34 -> x2, waiting for transfers between devices: 35.8 us -> 0.01 us  [on_device(): lax.ppermute(packed, 'tensor', [(i, i ^ step) for i in range(ways)])]
    ppermute x34 -> x2, starting transfers between devices: 30.3 us -> 2.62 us  [flip(): return lax.ppermute(x, 'chip', [(i, i ^ bit) for i in range(n)])]
  transfers between devices with their start and end apart: 102 -> 26, of which waited for: 38 -> 9; matrix products, arithmetic and copies ran while one was open for 33% -> 13% of each run, Pallas kernels for 0% -> 50%
where the time goes in v2:
time: 650 us; the launch traced here: 646 us
  Pallas kernels  343 us (53%)
  matrix products  90.7 us (14%)
  waiting for transfers between devices  75.1 us (12%)
  starting transfers between devices  65.2 us (10%)
  local copies, waits for them, and re-layouts  52.3 us (8%)
  other arithmetic  17.9 us (3%)
    pallas_call x2, Pallas kernels, gather_weights(): pl.pallas_call(functools.partial(gather_kernel, chips, ways, number), in_...  146 us
    pallas_call x2, Pallas kernels, scatter_grads(): pl.pallas_call(functools.partial(scatter_kernel, chips, ways, number), in...  142 us
    pallas_call x1, Pallas kernels, attention_backward(): pl.pallas_call(attention_backward_kernel, grid=(pairs,), in_specs=[pl.Blo...  35.3 us
    dot_general x4, matrix products, nn(): return jnp.dot(x, y, preferred_element_type=F32)  34.9 us
    ppermute x2, waiting for transfers between devices, to_owner(): lax.ppermute(work[:quarter], ('core', 'tensor'), moves(0))  29.6 us
    dot_general x8, matrix products, nt(): lax.dot_general(x, y, (((1,), (1,)), ((), ())), preferred_element_type=F32)  28.4 us
    dot_general x4, matrix products, tn(): lax.dot_general(x, y, (((0,), (0,)), ((), ())), preferred_element_type=F32)  27.4 us
    all_to_all x2, waiting for transfers between devices, to_owner(): lax.all_to_all(outgoing, dp, split_axis=0, concat_axis=0, tiled=True)  26 us
  transfers between devices with their start and end apart: 26, of which 9 were waited for; matrix products, arithmetic and copies ran while one was open for 13% of the time, Pallas kernels for 50%

profile of v2, /device:TPU:1, one launch (start us, length us, event | category | flops | bytes accessed | tf_op | source)
XLA Modules:
  0.0 646.0 jit_solution(13880041805244838871)
XLA Ops:
  7.9 5.4 all-to-all-start
  13.9 12.7 %all-to-all-done = bf16[8,72,1024]{2,1,0:T(8,128)(2,1)S(1)} async-done(((bf16[8,72,1024]{2,1,0:T(8,128)(2,1)}), bf16[8,72,1024]{2,1,0:T(8,128)(2,1)S(1)}, u32[]{:S(2)}, u32[]{:S(2)}) %all-to-all-start) | async-done | bytes 1179680 | tf_op jit(solution)/shard_map/all_to_all | solution.py:729
  29.6 7.9 %collective-permute-start = (bf16[288,1024]{1,0:T(8,128)(2,1)S(1)}, bf16[288,1024]{1,0:T(8,128)(2,1)S(1)}, u32[]{:S(2)}, u32[]{:S(2)}) collective-permute-start(bf16[288,1024]{1,0:T(8,128)(2,1)S(1)} %get-tuple-element.121), channel_id=1, source_target_pairs={{0,0},{1,1},{2,4},{3,5},{4,2},{5,3},{6,6},{7,7},{8,8},{9,9},{10,12... | collective-permute-start | bytes 1769480 | tf_op jit(solution)/shard_map/ppermute | solution.py:733
  38.6 19.0 %collective-permute-done = bf16[288,1024]{1,0:T(8,128)(2,1)S(1)} collective-permute-done((bf16[288,1024]{1,0:T(8,128)(2,1)S(1)}, bf16[288,1024]{1,0:T(8,128)(2,1)S(1)}, u32[]{:S(2)}, u32[]{:S(2)}) %collective-permute-start) | collective-permute-done | bytes 589856 | tf_op jit(solution)/shard_map/ppermute | solution.py:733
  60.6 47.8 %gather_weights.2 = bf16[2,2,256,1536]{3,2,1,0:T(8,128)(2,1)S(1)} custom-call(bf16[128,768]{1,0:T(8,128)(2,1)S(1)} %copy.69.refs_0_), custom_call_target="tpu_custom_call" | custom-call | tf_op jit(solution)/shard_map/gather_weights/pallas_call | solution.py:235
  110.1 98.2 %gather_weights.3 = (bf16[2,2,256,512]{3,2,1,0:T(8,128)(2,1)S(1)}, bf16[2,2,256,2048]{3,2,1,0:T(8,128)(2,1)S(1)}, bf16[2,2,256,2048]{3,2,1,0:T(8,128)(2,1)S(1)}) custom-call(bf16[128,256]{1,0:T(8,128)(2,1)S(1)} %bitcast.105, bf16[128,1024]{1,0:T(8,128)(2,1)S(1)} %copy-done.4, bf16[128,1024]{1,0:T(8,128)(2,1)S(1)} %bitcast.102), custom_call_target="tpu_custom_call" | custom-call | tf_op jit(solution)/shard_map/gather_weights/pallas_call | solution.py:235
  216.7 8.3 %fusion.4.qkv_ref = bf16[1152,1536]{1,0:T(8,128)(2,1)} fusion(bf16[1152,1024]{1,0:T(8,128)(2,1)} %constant_dynamic-update-slice_fusion.2, bf16[1024,1536]{1,0:T(8,128)(2,1)} %bitcast.98, f32[1536]{0:T(1024)S(1)} %add.232), kind=kOutput, calls=%fused_computation.18 | convolution fusion | flops 3627417600 | bytes 9050112 | tf_op jit(solution)/shard_map/dot_general | solution.py:656
  224.9 20.1 %attention_forward.1 = (bf16[1152,512]{1,0:T(8,128)(2,1)}, f32[4,2,1152]{2,1,0:T(2,128)}) custom-call(bf16[1152,1536]{1,0:T(8,128)(2,1)} %fusion.4.qkv_ref, s32[1152,1]{1,0:T(8,128)} %broadcast_in_dim.140.col_ref, s32[1,1152]{1,0:T(1,128)} %broadcast_in_dim.127.row_ref), custom_call_target="tpu_custom_call" | custom-call | flops 10871635968 | bytes 4718592 | tf_op jit(solution)/shard_map/attention_forward/pallas_call | solution.py:531
  248.4 4.1 collective-permute-done.4
  257.9 11.0 %multiply_convert_fusion = (bf16[1152,2048]{1,0:T(8,128)(2,1)S(1)}, f32[1152,2048]{1,0:T(8,128)}) fusion(f32[2048]{0:T(1024)S(1)} %bitcast.131, bf16[1024,2048]{1,0:T(8,128)(2,1)} %bitcast.107, bf16[576,1024]{1,0:T(8,128)(2,1)} %collective-permute-done.5, bf16[576,1024]{1,0:T(8,128)(2,1)S(1)} %fusion.20), kind=kOutput, calls=%fused_computation.14 | convolution fusion | flops 4850712576 | bytes 20717568 | tf_op jit(solution)/shard_map/dot_general | solution.py:656
  268.9 4.0 fusion.16
  276.8 3.7 all-to-all-start.2
  280.6 13.3 %all-to-all-done.2 = bf16[8,72,1024]{2,1,0:T(8,128)(2,1)S(1)} async-done(((bf16[8,72,1024]{2,1,0:T(8,128)(2,1)}), bf16[8,72,1024]{2,1,0:T(8,128)(2,1)S(1)}, u32[]{:S(2)}, u32[]{:S(2)}) %all-to-all-start.2) | async-done | bytes 1179680 | tf_op jit(solution)/shard_map/all_to_all | solution.py:729
  296.8 6.8 %collective-permute-start.9 = (bf16[288,1024]{1,0:T(8,128)(2,1)S(1)}, bf16[288,1024]{1,0:T(8,128)(2,1)S(1)}, u32[]{:S(2)}, u32[]{:S(2)}) collective-permute-start(bf16[288,1024]{1,0:T(8,128)(2,1)S(1)} %get-tuple-element.116), channel_id=1, source_target_pairs={{0,0},{1,1},{2,4},{3,5},{4,2},{5,3},{6,6},{7,7},{8,8},{9,9},{10,12... | collective-permute-start | bytes 1769480 | tf_op jit(solution)/shard_map/ppermute | solution.py:733
  306.1 6.7 %fusion.59 = (f32[576]{0:T(1024)S(1)}, f32[576,1024]{1,0:T(8,128)S(1)}) fusion(f32[1024]{0:T(1024)S(1)} %convert_element_type.86, f32[576,1024]{1,0:T(8,128)} %collective-permute-done.6, bf16[1024,2048]{1,0:T(8,128)(2,1)} %bitcast.110, bf16[1152,2048]{1,0:T(8,128)(2,1)} %copy-done.38, f32[1024]{0:T(1024)S(1)} %convert_element_type.83, ...), kind=kOutput, calls=%fused_computation.168 | convolution fusion | flops 2420637184 | bytes 13650688 | tf_op jit(solution)/shard_map/dot_general | solution.py:660
  313.2 10.7 %collective-permute-done.9 = bf16[288,1024]{1,0:T(8,128)(2,1)S(1)} collective-permute-done((bf16[288,1024]{1,0:T(8,128)(2,1)S(1)}, bf16[288,1024]{1,0:T(8,128)(2,1)S(1)}, u32[]{:S(2)}, u32[]{:S(2)}) %collective-permute-start.9) | collective-permute-done | bytes 589856 | tf_op jit(solution)/shard_map/ppermute | solution.py:733
  330.0 12.0 %fusion.52 = (f32[2048]{0:T(1024)S(1)}, bf16[1152,2048]{1,0:T(8,128)(2,1)S(1)}) fusion(f32[1152,2048]{1,0:T(8,128)} %get-tuple-element.143, bf16[1024,2048]{1,0:T(8,128)(2,1)S(1)} %bitcast.112, bf16[576,1024]{1,0:T(8,128)(2,1)S(1)} %collective-permute-done.11, bf16[576,1024]{1,0:T(8,128)(2,1)S(1)} %convert_element_type.91), kind=kOutput, calls=%fused_computation.161 | convolution fusion | flops 4862507008 | bytes 20717568 | tf_op jit(solution)/shard_map/dot_general | solution.py:656
  345.2 4.1 collective-permute-done.12
  355.5 11.6 %collective-permute-start.7 = (bf16[288,1024]{1,0:T(8,128)(2,1)}, bf16[288,1024]{1,0:T(8,128)(2,1)}, u32[]{:S(2)}, u32[]{:S(2)}) collective-permute-start(bf16[288,1024]{1,0:T(8,128)(2,1)} %get-tuple-element.118), channel_id=1, source_target_pairs={{0,0},{1,1},{4,2},{5,3},{2,4},{3,5},{6,6},{7,7},{8,8},{9,9},{12,10... | collective-permute-start | bytes 1769480 | tf_op jit(solution)/shard_map/ppermute | solution.py:743
  371.1 35.3 %attention_backward.1 = (bf16[1152,1536]{1,0:T(8,128)(2,1)}, f32[4,8,128]{2,1,0:T(8,128)}, f32[4,8,128]{2,1,0:T(8,128)}) custom-call(bf16[1152,1536]{1,0:T(8,128)(2,1)} %fusion.4.qkv_ref, bf16[1152,512]{1,0:T(8,128)(2,1)} %convolution_convert_fusion.3.do_ref, f32[4,2,1152]{2,1,0:T(2,128)} %get-tuple-element.31.lse_ref, s32[1152,1]{1,0:T(8,128)} %broadcast_in_dim.140.col_ref, ...), custom_call_target="tpu_custom_call" | custom-call | flops 27179089920 | bytes 8257536 | tf_op jit(solution)/shard_map/attention_backward/pallas_call | solution.py:595
  406.4 4.9 fusion.21
  417.6 5.8 gather_fusion.2
  423.4 4.9 all-to-all-start.1
  429.8 8.8 %convolution_convert_fusion.1 = bf16[1024,2048]{1,0:T(8,128)(2,1)S(1)} fusion(bf16[1152,2048]{1,0:T(8,128)(2,1)} %copy-done.38, bf16[576,1024]{1,0:T(8,128)(2,1)} %copy-done.37, bf16[576,1024]{1,0:T(8,128)(2,1)} %copy-done.21), kind=kOutput, calls=%fused_computation.20 | convolution fusion | flops 4838653952 | bytes 11272192 | tf_op jit(solution)/shard_map/dot_general | solution.py:664
  438.6 5.8 collective-permute-done.18
  449.5 4.6 collective-permute-start.15
  455.4 8.6 %convolution_convert_fusion = bf16[1024,2048]{1,0:T(8,128)(2,1)} fusion(bf16[1152,2048]{1,0:T(8,128)(2,1)S(1)} %bitcast.137, bf16[576,1024]{1,0:T(8,128)(2,1)} %collective-permute-done.5, bf16[576,1024]{1,0:T(8,128)(2,1)S(1)} %copy-done.18), kind=kOutput, calls=%fused_computation.19 | convolution fusion | flops 4838653952 | bytes 11272192 | tf_op jit(solution)/shard_map/dot_general | solution.py:664
  464.0 90.4 %scatter_grads.3 = (f32[128,1024]{1,0:T(8,128)S(1)}, f32[128,1024]{1,0:T(8,128)S(1)}) custom-call(bf16[2,2,256,2048]{3,2,1,0:T(8,128)(2,1)S(1)} %bitcast.94, bf16[2,2,256,2048]{3,2,1,0:T(8,128)(2,1)} %bitcast.118), custom_call_target="tpu_custom_call" | custom-call | tf_op jit(solution)/shard_map/scatter_grads/pallas_call | solution.py:482
  555.3 5.8 gather_fusion.3
  566.6 4.2 all-to-all-start.3
  570.8 7.2 %convolution_convert_fusion.2 = bf16[1024,1536]{1,0:T(8,128)(2,1)S(1)} fusion(bf16[1152,1024]{1,0:T(8,128)(2,1)} %constant_dynamic-update-slice_fusion.2, bf16[1152,1536]{1,0:T(8,128)(2,1)} %get-tuple-element.32), kind=kOutput, calls=%fused_computation.21 | convolution fusion | flops 3625451520 | bytes 9043968 | tf_op jit(solution)/shard_map/dot_general | solution.py:664
  584.3 51.2 %scatter_grads.2 = (f32[128,256]{1,0:T(8,128)S(1)}, f32[128,768]{1,0:T(8,128)S(1)}) custom-call(bf16[2,2,256,512]{3,2,1,0:T(8,128)(2,1)S(1)} %bitcast.103, bf16[2,2,256,1536]{3,2,1,0:T(8,128)(2,1)S(1)} %bitcast.101), custom_call_target="tpu_custom_call" | custom-call | tf_op jit(solution)/shard_map/scatter_grads/pallas_call | solution.py:482
  (245 shorter events, 99.5 us)
Async XLA Ops:
  7.9 18.7 %all-to-all-start = ((bf16[8,72,1024]{2,1,0:T(8,128)(2,1)}), bf16[8,72,1024]{2,1,0:T(8,128)(2,1)S(1)}, u32[]{:S(2)}, u32[]{:S(2)}) async-start(bf16[8,72,1024]{2,1,0:T(8,128)(2,1)} %bitcast.4), calls=%async_computation | async-start | bytes 2359296 | tf_op jit(solution)/shard_map/all_to_all | solution.py:729
  29.6 30.3 %copy-start.28 = (bf16[1024]{0:T(1024)(128)(2,1)S(1)}, bf16[1024]{0:T(1024)(128)(2,1)}, u32[]{:S(2)}) copy-start(bf16[1024]{0:T(1024)(128)(2,1)} %param.25) | copy-start | bytes 6148
  29.6 30.3 %copy-start.29 = (bf16[1024]{0:T(1024)(128)(2,1)S(1)}, bf16[1024]{0:T(1024)(128)(2,1)}, u32[]{:S(2)}) copy-start(bf16[1024]{0:T(1024)(128)(2,1)} %param.24) | copy-start | bytes 6148
  29.6 30.4 %copy-start.26 = (bf16[256,128]{1,0:T(8,128)(2,1)S(1)}, bf16[256,128]{1,0:T(8,128)(2,1)}, u32[]{:S(2)}) copy-start(bf16[256,128]{1,0:T(8,128)(2,1)} %param.26) | copy-start | bytes 196612
  29.6 30.5 %copy-start.23 = (bf16[3,128,256]{2,1,0:T(8,128)(2,1)S(1)}, bf16[3,128,256]{2,1,0:T(8,128)(2,1)}, u32[]{:S(2)}) copy-start(bf16[3,128,256]{2,1,0:T(8,128)(2,1)} %param.23) | copy-start | bytes 589828
  29.6 27.9 %collective-permute-start = (bf16[288,1024]{1,0:T(8,128)(2,1)S(1)}, bf16[288,1024]{1,0:T(8,128)(2,1)S(1)}, u32[]{:S(2)}, u32[]{:S(2)}) collective-permute-start(bf16[288,1024]{1,0:T(8,128)(2,1)S(1)} %get-tuple-element.121), channel_id=1, source_target_pairs={{0,0},{1,1},{2,4},{3,5},{4,2},{5,3},{6,6},{7,7},{8,8},{9,9},{10,12... | collective-permute-start | bytes 1769480 | tf_op jit(solution)/shard_map/ppermute | solution.py:733
  37.5 20.2 %collective-permute-start.1 = (bf16[288,1024]{1,0:T(8,128)(2,1)S(1)}, bf16[288,1024]{1,0:T(8,128)(2,1)S(1)}, u32[]{:S(2)}, u32[]{:S(2)}) collective-permute-start(bf16[288,1024]{1,0:T(8,128)(2,1)S(1)} %get-tuple-element.120), channel_id=1, source_target_pairs={{0,1},{1,0},{2,5},{3,4},{4,3},{5,2},{6,7},{7,6},{8,9},{9,8},{10,13... | collective-permute-start | bytes 1769480 | tf_op jit(solution)/shard_map/ppermute | solution.py:734
  59.3 155.0 %collective-permute-start.2 = (bf16[576,1024]{1,0:T(8,128)(2,1)S(1)}, bf16[576,1024]{1,0:T(8,128)(2,1)}, u32[]{:S(2)}, u32[]{:S(2)}) collective-permute-start(bf16[576,1024]{1,0:T(8,128)(2,1)S(1)} %get-tuple-element.122), channel_id=1, source_target_pairs={{0,4},{4,0},{1,5},{5,1},{2,6},{6,2},{3,7},{7,3},{8,12},{12,8},{9,1... | collective-permute-start | bytes 3538952 | tf_op jit(solution)/shard_map/ppermute | solution.py:21
  59.3 153.1 %collective-permute-start.3 = (s32[2,3]{1,0:T(2,128)S(1)}, s32[2,3]{1,0:T(2,128)S(1)}, u32[]{:S(2)}, u32[]{:S(2)}) collective-permute-start(s32[2,3]{1,0:T(2,128)S(1)} %bitcast.134), channel_id=1, source_target_pairs={{0,4},{4,0},{1,5},{5,1},{2,6},{6,2},{3,7},{7,3},{8,12},{12,8},{9,1... | collective-permute-start | bytes 80 | tf_op jit(solution)/shard_map/ppermute | solution.py:21
  60.2 49.8 %copy-start.4 = (bf16[128,1024]{1,0:T(8,128)(2,1)S(1)}, bf16[128,1024]{1,0:T(8,128)(2,1)}, u32[]{:S(2)}) copy-start(bf16[128,1024]{1,0:T(8,128)(2,1)} %refs_1_.1) | copy-start | bytes 786436
  247.1 5.4 collective-permute-start.4
  254.9 3.0 collective-permute-start.5
  273.0 33.2 %collective-permute-start.6 = (f32[576,1024]{1,0:T(8,128)}, f32[576,1024]{1,0:T(8,128)}, u32[]{:S(2)}, u32[]{:S(2)}) collective-permute-start(f32[576,1024]{1,0:T(8,128)} %fusion.16), channel_id=1, source_target_pairs={{0,4},{4,0},{1,5},{5,1},{2,6},{6,2},{3,7},{7,3},{8,12},{12,8},{9,1... | collective-permute-start | bytes 7077896 | tf_op jit(solution)/shard_map/ppermute | solution.py:21
  276.8 17.1 %all-to-all-start.2 = ((bf16[8,72,1024]{2,1,0:T(8,128)(2,1)}), bf16[8,72,1024]{2,1,0:T(8,128)(2,1)S(1)}, u32[]{:S(2)}, u32[]{:S(2)}) async-start(bf16[8,72,1024]{2,1,0:T(8,128)(2,1)} %bitcast.23), calls=%async_computation.2 | async-start | bytes 2359296 | tf_op jit(solution)/shard_map/all_to_all | solution.py:729
  296.8 27.1 %collective-permute-start.9 = (bf16[288,1024]{1,0:T(8,128)(2,1)S(1)}, bf16[288,1024]{1,0:T(8,128)(2,1)S(1)}, u32[]{:S(2)}, u32[]{:S(2)}) collective-permute-start(bf16[288,1024]{1,0:T(8,128)(2,1)S(1)} %get-tuple-element.116), channel_id=1, source_target_pairs={{0,0},{1,1},{2,4},{3,5},{4,2},{5,3},{6,6},{7,7},{8,8},{9,9},{10,12... | collective-permute-start | bytes 1769480 | tf_op jit(solution)/shard_map/ppermute | solution.py:733
  303.6 20.2 %collective-permute-start.10 = (bf16[288,1024]{1,0:T(8,128)(2,1)S(1)}, bf16[288,1024]{1,0:T(8,128)(2,1)S(1)}, u32[]{:S(2)}, u32[]{:S(2)}) collective-permute-start(bf16[288,1024]{1,0:T(8,128)(2,1)S(1)} %get-tuple-element.117), channel_id=1, source_target_pairs={{0,1},{1,0},{2,5},{3,4},{4,3},{5,2},{6,7},{7,6},{8,9},{9,8},{10,13... | collective-permute-start | bytes 1769480 | tf_op jit(solution)/shard_map/ppermute | solution.py:734
  327.1 2.9 collective-permute-start.11
  344.7 4.6 collective-permute-start.12
  353.8 13.7 %collective-permute-start.13 = (bf16[576,1024]{1,0:T(8,128)(2,1)S(1)}, bf16[576,1024]{1,0:T(8,128)(2,1)}, u32[]{:S(2)}, u32[]{:S(2)}) collective-permute-start(bf16[576,1024]{1,0:T(8,128)(2,1)S(1)} %convert_element_type.93), channel_id=1, source_target_pairs={{0,4},{4,0},{1,5},{5,1},{2,6},{6,2},{3,7},{7,3},{8,12},{12,8},{9,1... | collective-permute-start | bytes 3538952 | tf_op jit(solution)/shard_map/ppermute | solution.py:21
  355.5 59.7 %collective-permute-start.7 = (bf16[288,1024]{1,0:T(8,128)(2,1)}, bf16[288,1024]{1,0:T(8,128)(2,1)}, u32[]{:S(2)}, u32[]{:S(2)}) collective-permute-start(bf16[288,1024]{1,0:T(8,128)(2,1)} %get-tuple-element.118), channel_id=1, source_target_pairs={{0,0},{1,1},{4,2},{5,3},{2,4},{3,5},{6,6},{7,7},{8,8},{9,9},{12,10... | collective-permute-start | bytes 1769480 | tf_op jit(solution)/shard_map/ppermute | solution.py:743
  367.1 48.1 %collective-permute-start.8 = (bf16[288,1024]{1,0:T(8,128)(2,1)}, bf16[288,1024]{1,0:T(8,128)(2,1)}, u32[]{:S(2)}, u32[]{:S(2)}) collective-permute-start(bf16[288,1024]{1,0:T(8,128)(2,1)} %get-tuple-element.119), channel_id=1, source_target_pairs={{1,0},{0,1},{5,2},{4,3},{3,4},{2,5},{7,6},{6,7},{9,8},{8,9},{13,10... | collective-permute-start | bytes 1769480 | tf_op jit(solution)/shard_map/ppermute | solution.py:744
  371.1 35.3 %copy-start.3 = (bf16[2,2,256,1536]{3,2,1,0:T(8,128)(2,1)S(1)}, bf16[2,2,256,1536]{3,2,1,0:T(8,128)(2,1)}, u32[]{:S(2)}) copy-start(bf16[2,2,256,1536]{3,2,1,0:T(8,128)(2,1)} %copy-done.2) | copy-start | bytes 9437188
  411.3 34.3 %collective-permute-start.14 = (f32[576,1024]{1,0:T(8,128)}, f32[576,1024]{1,0:T(8,128)}, u32[]{:S(2)}, u32[]{:S(2)}) collective-permute-start(f32[576,1024]{1,0:T(8,128)} %fusion.21), channel_id=1, source_target_pairs={{0,4},{4,0},{1,5},{5,1},{2,6},{6,2},{3,7},{7,3},{8,12},{12,8},{9,1... | collective-permute-start | bytes 7077896 | tf_op jit(solution)/shard_map/ppermute | solution.py:21
  415.1 13.2 %collective-permute-start.17 = (f32[96,128]{1,0:T(8,128)S(1)}, f32[96,128]{1,0:T(8,128)S(1)}, u32[]{:S(2)}, u32[]{:S(2)}) collective-permute-start(f32[96,128]{1,0:T(8,128)S(1)} %bitcast.123), channel_id=1, source_target_pairs={{0,4},{4,0},{1,5},{5,1},{2,6},{6,2},{3,7},{7,3},{8,12},{12,8},{9,1... | collective-permute-start | bytes 147464 | tf_op jit(solution)/shard_map/ppermute | solution.py:21
  423.4 131.9 %all-to-all-start.1 = ((bf16[8,72,1024]{2,1,0:T(8,128)(2,1)}), bf16[8,72,1024]{2,1,0:T(8,128)(2,1)}, u32[]{:S(2)}, u32[]{:S(2)}) async-start(bf16[8,72,1024]{2,1,0:T(8,128)(2,1)} %bitcast.116), calls=%async_computation.1 | async-start | bytes 2359296 | tf_op jit(solution)/shard_map/all_to_all | solution.py:749
  428.3 16.1 %collective-permute-start.18 = (f32[96,128]{1,0:T(8,128)S(1)}, f32[96,128]{1,0:T(8,128)S(1)}, u32[]{:S(2)}, u32[]{:S(2)}) collective-permute-start(f32[96,128]{1,0:T(8,128)S(1)} %bitcast_add_fusion), channel_id=1, source_target_pairs={{0,8},{8,0},{16,24},{24,16},{1,9},{9,1},{17,25},{25,17},{2,10},{10... | collective-permute-start | bytes 147464 | tf_op jit(solution)/shard_map/ppermute | solution.py:26
  444.5 116.7 %collective-permute-start.19 = (f32[96,128]{1,0:T(8,128)S(1)}, f32[96,128]{1,0:T(8,128)}, u32[]{:S(2)}, u32[]{:S(2)}) collective-permute-start(f32[96,128]{1,0:T(8,128)S(1)} %fusion.78), channel_id=1, source_target_pairs={{0,16},{8,24},{16,0},{24,8},{1,17},{9,25},{17,1},{25,9},{2,18},{10... | collective-permute-start | bytes 147464 | tf_op jit(solution)/shard_map/ppermute | solution.py:26
  449.5 113.6 %collective-permute-start.15 = (bf16[288,1024]{1,0:T(8,128)(2,1)S(1)}, bf16[288,1024]{1,0:T(8,128)(2,1)S(1)}, u32[]{:S(2)}, u32[]{:S(2)}) collective-permute-start(bf16[288,1024]{1,0:T(8,128)(2,1)S(1)} %get-tuple-element.114), channel_id=1, source_target_pairs={{0,0},{1,1},{4,2},{5,3},{2,4},{3,5},{6,6},{7,7},{8,8},{9,9},{12,10... | collective-permute-start | bytes 1769480 | tf_op jit(solution)/shard_map/ppermute | solution.py:743
  454.1 109.0 %collective-permute-start.16 = (bf16[288,1024]{1,0:T(8,128)(2,1)S(1)}, bf16[288,1024]{1,0:T(8,128)(2,1)S(1)}, u32[]{:S(2)}, u32[]{:S(2)}) collective-permute-start(bf16[288,1024]{1,0:T(8,128)(2,1)S(1)} %get-tuple-element.115), channel_id=1, source_target_pairs={{1,0},{0,1},{5,2},{4,3},{3,4},{2,5},{7,6},{6,7},{9,8},{8,9},{13,10... | collective-permute-start | bytes 1769480 | tf_op jit(solution)/shard_map/ppermute | solution.py:744
  562.6 15.4 %collective-permute-start.20 = (f32[96,128]{1,0:T(8,128)}, f32[96,128]{1,0:T(8,128)S(1)}, u32[]{:S(2)}, u32[]{:S(2)}) collective-permute-start(f32[96,128]{1,0:T(8,128)} %add.277), channel_id=1, source_target_pairs={{0,1},{1,0},{2,3},{3,2},{4,5},{5,4},{6,7},{7,6},{8,9},{9,8},{10,11... | collective-permute-start | bytes 147464 | tf_op jit(solution)/shard_map/ppermute | solution.py:863
  566.6 71.9 %all-to-all-start.3 = ((bf16[8,72,1024]{2,1,0:T(8,128)(2,1)}), bf16[8,72,1024]{2,1,0:T(8,128)(2,1)S(1)}, u32[]{:S(2)}, u32[]{:S(2)}) async-start(bf16[8,72,1024]{2,1,0:T(8,128)(2,1)} %bitcast.117), calls=%async_computation.3 | async-start | bytes 2359296 | tf_op jit(solution)/shard_map/all_to_all | solution.py:749
  578.8 58.5 %collective-permute-start.21 = (f32[96,128]{1,0:T(8,128)S(1)}, f32[96,128]{1,0:T(8,128)S(1)}, u32[]{:S(2)}, u32[]{:S(2)}) collective-permute-start(f32[96,128]{1,0:T(8,128)S(1)} %add.278), channel_id=1, source_target_pairs={{0,2},{1,3},{2,0},{3,1},{4,6},{5,7},{6,4},{7,5},{8,10},{9,11},{10,... | collective-permute-start | bytes 147464 | tf_op jit(solution)/shard_map/ppermute | solution.py:863
  (37 other events, 319.2 us)
